TPU v7x, 1024 devices: a whole 4x4x32 slice. The times are simulated.
1024 devices in a mesh: dom: 256 (over z, x, core), sub: 4 (over y).
Axes of the slice: x: 4, y: 4, z: 32, core: 2. Of those that a mesh axis runs over, the one named last changes fastest.
Arguments:
- element_load: float32 [256, 8, 32, 8, 128], P('dom', None, 'sub'), may hold values from -48 to 48
- mobility: float32 [256, 8, 32, 8, 128], P('dom', None, 'sub'), may hold values from 0.5 to 4
- metric: float32 [3, 256, 32, 16], P(None, 'dom', 'sub'), may hold values from 0.5 to 2
Outputs:
- pressure: float32 [256, 8, 32, 8, 128], P('dom', None, 'sub')
- coarse_residual: float32 [256, 32, 17], P('dom', 'sub')
All inputs are finite; a program needn't handle non-finite values.
Results may differ from a plain program's by a relative error of at most 0.00008.
Values sent between devices are 32-bit elements; how exact they have to be, the bound alone decides.
A program may use at most 32 MiB of HBM per device.

v0:
```python
import jax
import jax.numpy as jnp
import numpy as np
from jax import lax
from jax.sharding import PartitionSpec as P

GLL_NODES = np.array(
    [
        -1.0,
        -0.8717401485096066,
        -0.5917001814331423,
        -0.2092992179024789,
        0.2092992179024789,
        0.5917001814331423,
        0.8717401485096066,
        1.0,
    ]
)
GLL_WEIGHTS = np.array(
    [
        0.03571428571428571,
        0.2107042271435061,
        0.3411226924835044,
        0.4124587946587038,
        0.4124587946587038,
        0.3411226924835044,
        0.2107042271435061,
        0.03571428571428571,
    ]
)
THETA = 1.65
DELTA = 1.35
RHO_FIRST = DELTA / THETA
RHO_SECOND = 1.0 / (2.0 * THETA / DELTA - RHO_FIRST)
EXACT = lax.Precision.HIGHEST


def extended(array, sides, width):
    for axis, dim in sides:
        size, length = (lax.axis_size(axis), array.shape[dim])
        up = [(i, (i + 1) % size) for i in range(size)]
        down = [(j, i) for i, j in up]
        last = lax.slice_in_dim(array, length - width, length, axis=dim)
        first = lax.slice_in_dim(array, 0, width, axis=dim)
        before = lax.ppermute(last, axis, up)
        after = lax.ppermute(first, axis, down)
        array = jnp.concatenate([before, array, after], axis=dim)
    return array


def passed_along(array, axis, by):
    size = lax.axis_size(axis)
    return lax.ppermute(array, axis, [(i, (i + by) % size) for i in range(size)])


def derivative_table():
    identity = np.eye(8)
    differences = GLL_NODES[:, None] - GLL_NODES[None, :] + identity
    barycentric = 1.0 / np.prod(differences, axis=1)
    matrix = barycentric[None, :] / barycentric[:, None] / differences
    matrix = matrix * (1.0 - identity)
    row_sums = np.sum(matrix, axis=1)
    return matrix - identity * row_sums[:, None]


def make_tables():
    derivative = jnp.asarray(derivative_table(), jnp.float32)
    weights = jnp.asarray(GLL_WEIGHTS, jnp.float32)
    coarse_basis = jnp.asarray(
        np.stack([(1.0 - GLL_NODES) / 8.0, (1.0 + GLL_NODES) / 8.0], axis=1), jnp.float32
    )
    return (derivative, weights, coarse_basis)


def kron_tables(derivative, coarse_basis, width):
    layers_z = width // 8
    identity = jnp.eye(layers_z, dtype=jnp.float32)
    deriv_z = jnp.kron(identity, derivative)
    squared_z = jnp.kron(identity, derivative * derivative)
    column = jnp.arange(width)
    source_cell = column[:, None]
    target_cell = column[None, :]
    joins = (
        (source_cell == target_cell)
        | (source_cell % 8 == 7) & (target_cell == source_cell + 1)
        | (source_cell % 8 == 0) & (target_cell == source_cell - 1)
    )
    face_sum_z = jnp.where(joins, 1.0, 0.0).astype(jnp.float32)
    vertex = jnp.arange(layers_z + 1)[None, :]
    cell_of = (column // 8)[:, None]
    lower_weight = jnp.tile(coarse_basis[:, 0], layers_z)[:, None]
    upper_weight = jnp.tile(coarse_basis[:, 1], layers_z)[:, None]
    restrict_z = jnp.where(vertex == cell_of, lower_weight, 0.0) + jnp.where(
        vertex == cell_of + 1, upper_weight, 0.0
    )
    return (deriv_z, squared_z, face_sum_z, restrict_z)


def point_factors(mobility, metric, weights):
    spread = jnp.repeat(metric, 8, axis=3)[:, :, None, :, None, :]
    layers_z = mobility.shape[-1] // 8
    z_weights = jnp.tile(weights, layers_z)
    quadrature = weights[:, None, None, None] * weights[None, None, :, None] * z_weights
    return spread * (mobility * quadrature)


def apply_local(values, factors, derivative, deriv_z):
    grad_x = jnp.einsum("ai,xiyjc->xayjc", derivative, values, precision=EXACT)
    grad_y = jnp.einsum("bj,xiyjc->xiybc", derivative, values, precision=EXACT)
    grad_z = jnp.dot(values, deriv_z.T, precision=EXACT)
    back_x = jnp.einsum("ai,xayjc->xiyjc", derivative, factors[0] * grad_x, precision=EXACT)
    back_y = jnp.einsum("bj,xiybc->xiyjc", derivative, factors[1] * grad_y, precision=EXACT)
    back_z = jnp.dot(factors[2] * grad_z, deriv_z, precision=EXACT)
    return back_x + back_y + back_z


def diagonal_of(factors, derivative, squared_z):
    squared = derivative * derivative
    part_x = jnp.einsum("ai,xayjc->xiyjc", squared, factors[0], precision=EXACT)
    part_y = jnp.einsum("bj,xiybc->xiyjc", squared, factors[1], precision=EXACT)
    part_z = jnp.dot(factors[2], squared_z, precision=EXACT)
    return part_x + part_y + part_z


def assemble(fields, face_sum_z):
    upper = fields[:, :, 7]
    bottom = fields[:, :, 0]
    rim_faces = jnp.stack([bottom[:, 0], upper[:, -1]])
    arrived_faces = extended(rim_faces, (("dom", 0),), 1)
    from_before = arrived_faces[0]
    from_after = arrived_faces[3]
    after_bottom = jnp.concatenate([bottom[:, 1:], from_after[:, None]], axis=1)
    before_upper = jnp.concatenate([from_before[:, None], upper[:, :-1]], axis=1)
    new_upper = upper + after_bottom
    new_bottom = bottom + before_upper
    fields = jnp.concatenate(
        [new_bottom[:, :, None], fields[:, :, 1:7], new_upper[:, :, None]], axis=2
    )
    upper = fields[:, :, :, :, 7]
    bottom = fields[:, :, :, :, 0]
    rim_faces = jnp.stack([bottom[:, :, :, 0], upper[:, :, :, -1]])
    arrived_faces = extended(rim_faces, (("sub", 0),), 1)
    from_before = arrived_faces[0]
    from_after = arrived_faces[3]
    after_bottom = jnp.concatenate([bottom[:, :, :, 1:], from_after[:, :, :, None]], axis=3)
    before_upper = jnp.concatenate([from_before[:, :, :, None], upper[:, :, :, :-1]], axis=3)
    new_upper = upper + after_bottom
    new_bottom = bottom + before_upper
    fields = jnp.concatenate(
        [new_bottom[:, :, :, :, None], fields[:, :, :, :, 1:7], new_upper[:, :, :, :, None]], axis=4
    )
    return jnp.dot(fields, face_sum_z, precision=EXACT)


def coarse_gather(source, coarse_basis, restrict_z):
    along_z = jnp.dot(source, restrict_z, precision=EXACT)
    corners = jnp.einsum("ip,jq,xiyjv->xpyqv", coarse_basis, coarse_basis, along_z, precision=EXACT)
    plane_pad = jnp.zeros_like(corners[:1, 0])
    planes = jnp.concatenate([corners[:, 0], plane_pad], axis=0) + jnp.concatenate(
        [plane_pad, corners[:, 1]], axis=0
    )
    arriving = passed_along(planes[-1], "dom", 1)
    planes = jnp.concatenate([planes[:1] + arriving[None], planes[1:-1]], axis=0)
    row_pad = jnp.zeros_like(planes[:, :1, 0])
    lines = jnp.concatenate([planes[:, :, 0], row_pad], axis=1) + jnp.concatenate(
        [row_pad, planes[:, :, 1]], axis=1
    )
    arriving_y = passed_along(lines[:, -1], "sub", 1)
    return jnp.concatenate([lines[:, :1] + arriving_y[:, None], lines[:, 1:-1]], axis=1)


def shards(element_load, mobility, metric):
    derivative, weights, coarse_basis = make_tables()
    width = element_load.shape[-1]
    deriv_z, squared_z, face_sum_z, restrict_z = kron_tables(derivative, coarse_basis, width)
    factors = point_factors(mobility, metric, weights)
    diag_local = diagonal_of(factors, derivative, squared_z)
    assembled = assemble(jnp.stack([element_load, diag_local]), face_sum_z)
    right_side = assembled[0]
    inverse = 1.0 / assembled[1]
    first_step = inverse * right_side / THETA
    resid_first = (
        right_side
        - assemble(apply_local(first_step, factors, derivative, deriv_z)[None], face_sum_z)[0]
    )
    pressure = first_step + (
        RHO_SECOND * RHO_FIRST * first_step + 2.0 * RHO_SECOND / DELTA * (inverse * resid_first)
    )
    final_local = element_load - apply_local(pressure, factors, derivative, deriv_z)
    return (pressure, coarse_gather(final_local, coarse_basis, restrict_z))


def solution(mesh):
    in_specs = (
        P("dom", None, "sub", None, None),
        P("dom", None, "sub", None, None),
        P(None, "dom", "sub", None),
    )
    out_specs = (P("dom", None, "sub", None, None), P("dom", "sub", None))
    return jax.shard_map(shards, mesh=mesh, in_specs=in_specs, out_specs=out_specs, check_vma=False)
```

profile of v0, /device:TPU:24, one launch (start us, length us, event | category | flops | bytes accessed | tf_op | source)
XLA Modules:
  0.0 97.7 jit_solution(717529640062284788)
XLA Ops:
  0.7 0.6 copy-done.5
  1.5 1.0 %multiply_bitcast_fusion = f32[8,8,8,128]{3,2,1,0:T(8,128)S(1)} fusion(f32[1,8,8,8,128]{4,3,2,1,0:T(8,128)} %param.7, f32[8,8,128]{2,1,0:T(8,128)S(1)} %broadcast_multiply_fusion.3), kind=kLoop, calls=%fused_computation.68 | loop fusion | flops 65536 | bytes 557056 | tf_op jit(solution)/shard_map/mul | solution.py:104
  2.7 0.5 copy-done.4
  3.5 0.5 copy-done.6
  5.2 0.6 copy-done.1
  6.0 0.5 copy-done.3
  7.4 20.3 %collective-permute-start.1 = (f32[1,2,8,8,128]{4,3,2,1,0:T(8,128)S(1)}, f32[1,2,8,8,128]{4,3,2,1,0:T(8,128)S(1)}, u32[]{:S(2)}, u32[]{:S(2)}) collective-permute-start(f32[1,2,8,8,128]{4,3,2,1,0:T(8,128)S(1)} %bitcast.301), channel_id=1, source_target_pairs={{4,0},{8,4},{12,8},{16,12},{20,16},{24,20},{28,24},{32,28},{36,32}... | collective-permute-start | bytes 196616 | tf_op jit(solution)/shard_map/ppermute | solution.py:46
  27.7 1.9 %collective-permute-done.1 = f32[1,2,8,8,128]{4,3,2,1,0:T(8,128)S(1)} collective-permute-done((f32[1,2,8,8,128]{4,3,2,1,0:T(8,128)S(1)}, f32[1,2,8,8,128]{4,3,2,1,0:T(8,128)S(1)}, u32[]{:S(2)}, u32[]{:S(2)}) %collective-permute-start.1) | collective-permute-done | bytes 65568 | tf_op jit(solution)/shard_map/ppermute | solution.py:46
  29.7 1.9 %collective-permute-start = (f32[1,2,8,8,128]{4,3,2,1,0:T(8,128)S(1)}, f32[1,2,8,8,128]{4,3,2,1,0:T(8,128)S(1)}, u32[]{:S(2)}, u32[]{:S(2)}) collective-permute-start(f32[1,2,8,8,128]{4,3,2,1,0:T(8,128)S(1)} %bitcast.318), channel_id=1, source_target_pairs={{0,4},{4,8},{8,12},{12,16},{16,20},{20,24},{24,28},{28,32},{32,36}... | collective-permute-start | bytes 196616 | tf_op jit(solution)/shard_map/ppermute | solution.py:45
  31.6 7.0 %collective-permute-done = f32[1,2,8,8,128]{4,3,2,1,0:T(8,128)S(1)} collective-permute-done((f32[1,2,8,8,128]{4,3,2,1,0:T(8,128)S(1)}, f32[1,2,8,8,128]{4,3,2,1,0:T(8,128)S(1)}, u32[]{:S(2)}, u32[]{:S(2)}) %collective-permute-start) | collective-permute-done | bytes 65568 | tf_op jit(solution)/shard_map/ppermute | solution.py:45
  38.9 2.7 %collective-permute-start.3 = (f32[1,2,1,8,128]{4,3,1,2,0:T(8,128)S(1)}, f32[1,2,1,8,128]{4,3,1,2,0:T(8,128)S(1)}, u32[]{:S(2)}, u32[]{:S(2)}) collective-permute-start(f32[1,2,1,8,128]{4,3,1,2,0:T(8,128)S(1)} %slice_bitcast_fusion.9), channel_id=1, source_target_pairs={{1,0},{2,1},{3,2},{0,3},{5,4},{6,5},{7,6},{4,7},{9,8},{10,9},{11,1... | collective-permute-start | bytes 24584 | tf_op jit(solution)/shard_map/ppermute | solution.py:46
  42.1 3.6 %collective-permute-done.3 = f32[1,2,1,8,128]{4,3,1,2,0:T(8,128)S(1)} collective-permute-done((f32[1,2,1,8,128]{4,3,1,2,0:T(8,128)S(1)}, f32[1,2,1,8,128]{4,3,1,2,0:T(8,128)S(1)}, u32[]{:S(2)}, u32[]{:S(2)}) %collective-permute-start.3) | collective-permute-done | bytes 8224 | tf_op jit(solution)/shard_map/ppermute | solution.py:46
  45.7 1.9 %collective-permute-start.2 = (f32[1,2,1,8,128]{4,3,1,2,0:T(8,128)S(1)}, f32[1,2,1,8,128]{4,3,1,2,0:T(8,128)S(1)}, u32[]{:S(2)}, u32[]{:S(2)}) collective-permute-start(f32[1,2,1,8,128]{4,3,1,2,0:T(8,128)S(1)} %slice_bitcast_fusion.10), channel_id=1, source_target_pairs={{0,1},{1,2},{2,3},{3,0},{4,5},{5,6},{6,7},{7,4},{8,9},{9,10},{10,1... | collective-permute-start | bytes 24584 | tf_op jit(solution)/shard_map/ppermute | solution.py:45
  47.6 3.6 %collective-permute-done.2 = f32[1,2,1,8,128]{4,3,1,2,0:T(8,128)S(1)} collective-permute-done((f32[1,2,1,8,128]{4,3,1,2,0:T(8,128)S(1)}, f32[1,2,1,8,128]{4,3,1,2,0:T(8,128)S(1)}, u32[]{:S(2)}, u32[]{:S(2)}) %collective-permute-start.2) | collective-permute-done | bytes 8224 | tf_op jit(solution)/shard_map/ppermute | solution.py:45
  51.3 0.7 fusion.21
  52.0 0.6 copy-done.2
  55.0 0.5 fusion.7
  55.6 1.9 %collective-permute-start.5 = (f32[1,1,8,8,128]{4,3,2,1,0:T(8,128)S(1)}, f32[1,1,8,8,128]{4,3,2,1,0:T(8,128)S(1)}, u32[]{:S(2)}, u32[]{:S(2)}) collective-permute-start(f32[1,1,8,8,128]{4,3,2,1,0:T(8,128)S(1)} %bitcast.306), channel_id=1, source_target_pairs={{4,0},{8,4},{12,8},{16,12},{20,16},{24,20},{28,24},{32,28},{36,32}... | collective-permute-start | bytes 98312 | tf_op jit(solution)/shard_map/ppermute | solution.py:46
  57.5 2.4 %collective-permute-start.4 = (f32[1,1,8,8,128]{4,3,2,1,0:T(8,128)S(1)}, f32[1,1,8,8,128]{4,3,2,1,0:T(8,128)S(1)}, u32[]{:S(2)}, u32[]{:S(2)}) collective-permute-start(f32[1,1,8,8,128]{4,3,2,1,0:T(8,128)S(1)} %bitcast.308), channel_id=1, source_target_pairs={{0,4},{4,8},{8,12},{12,16},{16,20},{20,24},{24,28},{28,32},{32,36}... | collective-permute-start | bytes 98312 | tf_op jit(solution)/shard_map/ppermute | solution.py:45
  60.0 0.6 copy-done.9
  60.7 5.3 %collective-permute-done.4 = f32[1,1,8,8,128]{4,3,2,1,0:T(8,128)S(1)} collective-permute-done((f32[1,1,8,8,128]{4,3,2,1,0:T(8,128)S(1)}, f32[1,1,8,8,128]{4,3,2,1,0:T(8,128)S(1)}, u32[]{:S(2)}, u32[]{:S(2)}) %collective-permute-start.4) | collective-permute-done | bytes 32800 | tf_op jit(solution)/shard_map/ppermute | solution.py:45
  66.1 3.1 %collective-permute-start.6 = (f32[1,1,1,8,128]{4,3,2,1,0:T(8,128)S(1)}, f32[1,1,1,8,128]{4,3,2,1,0:T(8,128)S(1)}, u32[]{:S(2)}, u32[]{:S(2)}) collective-permute-start(f32[1,1,1,8,128]{4,3,2,1,0:T(8,128)S(1)} %slice_bitcast_fusion.12), channel_id=1, source_target_pairs={{0,1},{1,2},{2,3},{3,0},{4,5},{5,6},{6,7},{7,4},{8,9},{9,10},{10,1... | collective-permute-start | bytes 12296 | tf_op jit(solution)/shard_map/ppermute | solution.py:45
  69.2 2.4 %collective-permute-done.6 = f32[1,1,1,8,128]{4,3,2,1,0:T(8,128)S(1)} collective-permute-done((f32[1,1,1,8,128]{4,3,2,1,0:T(8,128)S(1)}, f32[1,1,1,8,128]{4,3,2,1,0:T(8,128)S(1)}, u32[]{:S(2)}, u32[]{:S(2)}) %collective-permute-start.6) | collective-permute-done | bytes 4128 | tf_op jit(solution)/shard_map/ppermute | solution.py:45
  71.6 1.9 %collective-permute-start.7 = (f32[1,1,1,8,128]{4,3,2,1,0:T(8,128)S(1)}, f32[1,1,1,8,128]{4,3,2,1,0:T(8,128)S(1)}, u32[]{:S(2)}, u32[]{:S(2)}) collective-permute-start(f32[1,1,1,8,128]{4,3,2,1,0:T(8,128)S(1)} %slice_bitcast_fusion.11), channel_id=1, source_target_pairs={{1,0},{2,1},{3,2},{0,3},{5,4},{6,5},{7,6},{4,7},{9,8},{10,9},{11,1... | collective-permute-start | bytes 12296 | tf_op jit(solution)/shard_map/ppermute | solution.py:46
  73.6 4.8 %collective-permute-done.7 = f32[1,1,1,8,128]{4,3,2,1,0:T(8,128)S(1)} collective-permute-done((f32[1,1,1,8,128]{4,3,2,1,0:T(8,128)S(1)}, f32[1,1,1,8,128]{4,3,2,1,0:T(8,128)S(1)}, u32[]{:S(2)}, u32[]{:S(2)}) %collective-permute-start.7) | collective-permute-done | bytes 4128 | tf_op jit(solution)/shard_map/ppermute | solution.py:46
  78.4 0.5 fusion.12
  81.3 0.6 fusion.18
  83.4 1.9 %collective-permute-start.8 = (f32[8,2,17]{2,1,0:T(2,128)S(1)}, f32[8,2,17]{2,1,0:T(2,128)S(1)}, u32[]{:S(2)}, u32[]{:S(2)}) collective-permute-start(f32[8,2,17]{2,1,0:T(2,128)S(1)} %fusion.75), channel_id=1, source_target_pairs={{0,4},{4,8},{8,12},{12,16},{16,20},{20,24},{24,28},{28,32},{32,36}... | collective-permute-start | bytes 3272 | tf_op jit(solution)/shard_map/ppermute | solution.py:53
  85.3 6.4 %collective-permute-done.8 = f32[8,2,17]{2,1,0:T(2,128)S(1)} collective-permute-done((f32[8,2,17]{2,1,0:T(2,128)S(1)}, f32[8,2,17]{2,1,0:T(2,128)S(1)}, u32[]{:S(2)}, u32[]{:S(2)}) %collective-permute-start.8) | collective-permute-done | bytes 1120 | tf_op jit(solution)/shard_map/ppermute | solution.py:53
  91.7 3.1 %collective-permute-start.9 = (f32[1,17]{1,0:T(1,128)S(1)}, f32[1,17]{1,0:T(1,128)S(1)}, u32[]{:S(2)}, u32[]{:S(2)}) collective-permute-start(f32[1,17]{1,0:T(1,128)S(1)} %add_bitcast_fusion), channel_id=1, source_target_pairs={{0,1},{1,2},{2,3},{3,0},{4,5},{5,6},{6,7},{7,4},{8,9},{9,10},{10,1... | collective-permute-start | bytes 212 | tf_op jit(solution)/shard_map/ppermute | solution.py:53
  94.8 2.3 %collective-permute-done.9 = f32[1,17]{1,0:T(1,128)S(1)} collective-permute-done((f32[1,17]{1,0:T(1,128)S(1)}, f32[1,17]{1,0:T(1,128)S(1)}, u32[]{:S(2)}, u32[]{:S(2)}) %collective-permute-start.9) | collective-permute-done | bytes 100 | tf_op jit(solution)/shard_map/ppermute | solution.py:53
  97.1 0.6 pad_maximum_fusion.4
  (88 shorter events, 10.1 us)
Async XLA Ops:
  0.6 0.7 copy-start.5
  2.5 0.7 copy-start.4
  3.3 0.7 copy-start.6
  3.3 0.7 copy-start.7
  4.9 1.0 copy-start.1
  5.8 0.7 copy-start.3
  7.4 22.2 %collective-permute-start.1 = (f32[1,2,8,8,128]{4,3,2,1,0:T(8,128)S(1)}, f32[1,2,8,8,128]{4,3,2,1,0:T(8,128)S(1)}, u32[]{:S(2)}, u32[]{:S(2)}) collective-permute-start(f32[1,2,8,8,128]{4,3,2,1,0:T(8,128)S(1)} %bitcast.301), channel_id=1, source_target_pairs={{4,0},{8,4},{12,8},{16,12},{20,16},{24,20},{28,24},{32,28},{36,32}... | collective-permute-start | bytes 196616 | tf_op jit(solution)/shard_map/ppermute | solution.py:46
  29.7 9.0 %collective-permute-start = (f32[1,2,8,8,128]{4,3,2,1,0:T(8,128)S(1)}, f32[1,2,8,8,128]{4,3,2,1,0:T(8,128)S(1)}, u32[]{:S(2)}, u32[]{:S(2)}) collective-permute-start(f32[1,2,8,8,128]{4,3,2,1,0:T(8,128)S(1)} %bitcast.318), channel_id=1, source_target_pairs={{0,4},{4,8},{8,12},{12,16},{16,20},{20,24},{24,28},{28,32},{32,36}... | collective-permute-start | bytes 196616 | tf_op jit(solution)/shard_map/ppermute | solution.py:45
  38.9 6.8 %collective-permute-start.3 = (f32[1,2,1,8,128]{4,3,1,2,0:T(8,128)S(1)}, f32[1,2,1,8,128]{4,3,1,2,0:T(8,128)S(1)}, u32[]{:S(2)}, u32[]{:S(2)}) collective-permute-start(f32[1,2,1,8,128]{4,3,1,2,0:T(8,128)S(1)} %slice_bitcast_fusion.9), channel_id=1, source_target_pairs={{1,0},{2,1},{3,2},{0,3},{5,4},{6,5},{7,6},{4,7},{9,8},{10,9},{11,1... | collective-permute-start | bytes 24584 | tf_op jit(solution)/shard_map/ppermute | solution.py:46
  45.7 5.5 %collective-permute-start.2 = (f32[1,2,1,8,128]{4,3,1,2,0:T(8,128)S(1)}, f32[1,2,1,8,128]{4,3,1,2,0:T(8,128)S(1)}, u32[]{:S(2)}, u32[]{:S(2)}) collective-permute-start(f32[1,2,1,8,128]{4,3,1,2,0:T(8,128)S(1)} %slice_bitcast_fusion.10), channel_id=1, source_target_pairs={{0,1},{1,2},{2,3},{3,0},{4,5},{5,6},{6,7},{7,4},{8,9},{9,10},{10,1... | collective-permute-start | bytes 24584 | tf_op jit(solution)/shard_map/ppermute | solution.py:45
  52.0 0.7 copy-start.2
  55.6 5.2 %collective-permute-start.5 = (f32[1,1,8,8,128]{4,3,2,1,0:T(8,128)S(1)}, f32[1,1,8,8,128]{4,3,2,1,0:T(8,128)S(1)}, u32[]{:S(2)}, u32[]{:S(2)}) collective-permute-start(f32[1,1,8,8,128]{4,3,2,1,0:T(8,128)S(1)} %bitcast.306), channel_id=1, source_target_pairs={{4,0},{8,4},{12,8},{16,12},{20,16},{24,20},{28,24},{32,28},{36,32}... | collective-permute-start | bytes 98312 | tf_op jit(solution)/shard_map/ppermute | solution.py:46
  57.5 2.4 %copy-start.10 = (f32[8]{0:T(128)S(1)}, f32[8]{0:T(128)}, u32[]{:S(2)}) copy-start(f32[8]{0:T(128)} %constant.79) | copy-start | bytes 100
  57.5 8.6 %collective-permute-start.4 = (f32[1,1,8,8,128]{4,3,2,1,0:T(8,128)S(1)}, f32[1,1,8,8,128]{4,3,2,1,0:T(8,128)S(1)}, u32[]{:S(2)}, u32[]{:S(2)}) collective-permute-start(f32[1,1,8,8,128]{4,3,2,1,0:T(8,128)S(1)} %bitcast.308), channel_id=1, source_target_pairs={{0,4},{4,8},{8,12},{12,16},{16,20},{20,24},{24,28},{28,32},{32,36}... | collective-permute-start | bytes 98312 | tf_op jit(solution)/shard_map/ppermute | solution.py:45
  59.9 0.7 copy-start.9
  66.1 5.5 %collective-permute-start.6 = (f32[1,1,1,8,128]{4,3,2,1,0:T(8,128)S(1)}, f32[1,1,1,8,128]{4,3,2,1,0:T(8,128)S(1)}, u32[]{:S(2)}, u32[]{:S(2)}) collective-permute-start(f32[1,1,1,8,128]{4,3,2,1,0:T(8,128)S(1)} %slice_bitcast_fusion.12), channel_id=1, source_target_pairs={{0,1},{1,2},{2,3},{3,0},{4,5},{5,6},{6,7},{7,4},{8,9},{9,10},{10,1... | collective-permute-start | bytes 12296 | tf_op jit(solution)/shard_map/ppermute | solution.py:45
  71.6 6.7 %collective-permute-start.7 = (f32[1,1,1,8,128]{4,3,2,1,0:T(8,128)S(1)}, f32[1,1,1,8,128]{4,3,2,1,0:T(8,128)S(1)}, u32[]{:S(2)}, u32[]{:S(2)}) collective-permute-start(f32[1,1,1,8,128]{4,3,2,1,0:T(8,128)S(1)} %slice_bitcast_fusion.11), channel_id=1, source_target_pairs={{1,0},{2,1},{3,2},{0,3},{5,4},{6,5},{7,6},{4,7},{9,8},{10,9},{11,1... | collective-permute-start | bytes 12296 | tf_op jit(solution)/shard_map/ppermute | solution.py:46
  79.0 1.0 %copy-start = (f32[1,8,8,8,128]{4,3,2,1,0:T(8,128)}, f32[1,8,8,8,128]{4,3,2,1,0:T(8,128)S(1)}, u32[]{:S(2)}) copy-start(f32[1,8,8,8,128]{4,3,2,1,0:T(8,128)S(1)} %fusion.12) | copy-start | bytes 786436
  81.9 0.7 copy-start.8
  83.4 8.3 %collective-permute-start.8 = (f32[8,2,17]{2,1,0:T(2,128)S(1)}, f32[8,2,17]{2,1,0:T(2,128)S(1)}, u32[]{:S(2)}, u32[]{:S(2)}) collective-permute-start(f32[8,2,17]{2,1,0:T(2,128)S(1)} %fusion.75), channel_id=1, source_target_pairs={{0,4},{4,8},{8,12},{12,16},{16,20},{20,24},{24,28},{28,32},{32,36}... | collective-permute-start | bytes 3272 | tf_op jit(solution)/shard_map/ppermute | solution.py:53
  91.7 5.5 %collective-permute-start.9 = (f32[1,17]{1,0:T(1,128)S(1)}, f32[1,17]{1,0:T(1,128)S(1)}, u32[]{:S(2)}, u32[]{:S(2)}) collective-permute-start(f32[1,17]{1,0:T(1,128)S(1)} %add_bitcast_fusion), channel_id=1, source_target_pairs={{0,1},{1,2},{2,3},{3,0},{4,5},{5,6},{6,7},{7,4},{8,9},{9,10},{10,1... | collective-permute-start | bytes 212 | tf_op jit(solution)/shard_map/ppermute | solution.py:53
where the time goes:
time: 98.4 us; the launch traced here: 97.7 us
  starting transfers between devices  41.2 us (42%)
  waiting for transfers between devices  37.2 us (38%)
  matrix products  8.94 us (9%)
  local copies, waits for them, and re-layouts  6.22 us (6%)
  other arithmetic  2.95 us (3%)
  between operations  1.25 us (1%)
    ppermute x4, starting transfers between devices, extended(): after = lax.ppermute(first, axis, down)  26.8 us
    ppermute x4, waiting for transfers between devices, extended(): before = lax.ppermute(last, axis, up)  18.3 us
    ppermute x4, waiting for transfers between devices, extended(): after = lax.ppermute(first, axis, down)  10.2 us
    ppermute x4, starting transfers between devices, extended(): before = lax.ppermute(last, axis, up)  9.38 us
    ppermute x2, waiting for transfers between devices, passed_along(): lax.ppermute(array, axis, [(i, (i + by) % size) for i in range(size)])  8.67 us
    ppermute x2, starting transfers between devices, passed_along(): lax.ppermute(array, axis, [(i, (i + by) % size) for i in range(size)])  5.05 us
    unnamed x24, local copies, waits for them, and re-layouts  4.4 us
  transfers between devices with their start and end apart: 10, of which 9 were waited for; matrix products, arithmetic and copies ran while one was open for 1% of the time, Pallas kernels for 0%

commit v1 on v0

v1 whole, which is shorter than its diff:
```python
import jax
import jax.numpy as jnp
import numpy as np
from jax import lax
from jax.experimental import pallas as pl
from jax.experimental.pallas import tpu as pltpu
from jax.sharding import PartitionSpec as P

NODES = np.array(
    [
        -1.0,
        -0.8717401485096066,
        -0.5917001814331423,
        -0.2092992179024789,
        0.2092992179024789,
        0.5917001814331423,
        0.8717401485096066,
        1.0,
    ]
)
WEIGHTS = np.array(
    [
        0.03571428571428571,
        0.2107042271435061,
        0.3411226924835044,
        0.4124587946587038,
        0.4124587946587038,
        0.3411226924835044,
        0.2107042271435061,
        0.03571428571428571,
    ]
)
THETA = 1.65
DELTA = 1.35
RHO_FIRST = DELTA / THETA
RHO_SECOND = 1.0 / (2.0 * THETA / DELTA - RHO_FIRST)
KEEP = float(1.0 + RHO_SECOND * RHO_FIRST)
STEP = float(2.0 * RHO_SECOND / DELTA)
MESH = pl.DeviceIdType.MESH
F32 = jnp.float32
BF16 = jnp.bfloat16


def derivative_table():
    identity = np.eye(8)
    differences = NODES[:, None] - NODES[None, :] + identity
    barycentric = 1.0 / np.prod(differences, axis=1)
    matrix = barycentric[None, :] / barycentric[:, None] / differences
    matrix = matrix * (1.0 - identity)
    row_sums = np.sum(matrix, axis=1)
    return matrix - identity * row_sums[:, None]


DERIV = derivative_table()


def small_tables():
    deriv = DERIV.astype(np.float32).astype(np.float64)
    lower = (1.0 - NODES) / 8.0
    rows = [
        np.broadcast_to(np.tile(WEIGHTS, 16)[None, :], (8, 128)),
        np.tile(deriv.T, (1, 16)),
        np.tile(deriv, (1, 16)),
        np.tile(deriv * deriv, (1, 16)),
        np.broadcast_to(lower[:, None], (8, 128)),
    ]
    return np.stack(rows).astype(np.float32)


def total(terms):
    while len(terms) > 1:
        terms = [a + b for a, b in zip(terms[0::2], terms[1::2])] + (
            [terms[-1]] if len(terms) % 2 else []
        )
    return terms[0]


def apply_line(matrix, v, sign):
    even = [v[m] + v[7 - m] for m in range(4)]
    odd = [v[m] - v[7 - m] for m in range(4)]
    out = [None] * 8
    for a in range(4):
        with_even = total(
            [float((matrix[a, m] + matrix[a, 7 - m]) / 2) * even[m] for m in range(4)]
        )
        with_odd = total([float((matrix[a, m] - matrix[a, 7 - m]) / 2) * odd[m] for m in range(4)])
        out[a] = with_odd + with_even
        out[7 - a] = with_odd - with_even if sign < 0 else with_even - with_odd
    return out


def halves(x):
    high = x.astype(BF16)
    low = (x - high.astype(F32)).astype(BF16)
    return high, low


def wide_dot(x, table):
    high, low = halves(x)
    both = jnp.dot(jnp.concatenate([high, low], axis=1), table, preferred_element_type=F32)
    return both[:, :128] + both[:, 128:]


def kernel(
    load_hbm, mob_hbm, met_hbm, tab_hbm,
    press_hbm, coarse_ref,
    load_v, mob_v, met_v, tab_v, mats,
    fx, fy, fz, dg, rhs, fs, kv, zz, pr, out_v,
    sya, syb, sc,
    rxl, rxd, rya, rca, rxb, ryb, rcb, rc,
    local_sem, send_sem, recv_sem,
):
    d, s = lax.axis_index("dom"), lax.axis_index("sub")
    nd, ns = lax.axis_size("dom"), lax.axis_size("sub")
    dn, dp = lax.rem(d + 1, nd), lax.rem(d + nd - 1, nd)
    sn, sp = lax.rem(s + 1, ns), lax.rem(s + ns - 1, ns)

    fetch = [
        pltpu.make_async_copy(met_hbm, met_v, local_sem.at[0]),
        pltpu.make_async_copy(tab_hbm, tab_v, local_sem.at[1]),
        pltpu.make_async_copy(mob_hbm.at[0], mob_v, local_sem.at[2]),
        pltpu.make_async_copy(load_hbm.at[0], load_v, local_sem.at[3]),
    ]
    for copy in fetch:
        copy.start()
    barrier = pltpu.get_barrier_semaphore()
    around = [(a, b) for a in (dp, d, dn) for b in (sp, s, sn) if not (a is d and b is s)]
    for device in around:
        pl.semaphore_signal(barrier, inc=1, device_id=device, device_id_type=MESH)

    lane = lax.broadcasted_iota(jnp.int32, (8, 128), 1)
    sub8 = lax.broadcasted_iota(jnp.int32, (8, 128), 0)
    to_right = (lane % 8 == 7) & (lane != 127)
    to_left = (lane % 8 == 0) & (lane != 0)

    def z_joined(v):
        moved = jnp.where(to_right, pltpu.roll(v, 127, 1), pltpu.roll(v, 1, 1))
        return v + jnp.where(to_right | to_left, moved, 0.0)

    fetch[0].wait()
    fetch[1].wait()
    big_row = lax.broadcasted_iota(jnp.int32, (128, 128), 0)
    big_lane = lax.broadcasted_iota(jnp.int32, (128, 128), 1)
    same_cell = big_row // 8 == big_lane // 8

    def put_matrix(slot, matrix):
        high, low = halves(matrix)
        mats[slot, 0:128, 0:128] = high
        mats[slot, 0:128, 128:256] = low
        mats[slot, 128:256, 0:128] = high
        mats[slot, 128:256, 128:256] = jnp.zeros((128, 128), BF16)

    def tall(tile):
        return jnp.broadcast_to(tile[None], (16, 8, 128)).reshape(128, 128)

    for slot in range(3):
        put_matrix(slot, jnp.where(same_cell, tall(tab_v[1 + slot]), 0.0))
    lower = tall(tab_v[4])
    at_low, at_high = big_lane == big_row // 8, big_lane == big_row // 8 + 1
    put_matrix(3, jnp.where(at_low, lower, jnp.where(at_high, 0.25 - lower, 0.0)))
    put_matrix(4, jnp.where(at_low, -0.125, jnp.where(at_high, 0.125, 0.0)))

    cell_of = lax.broadcasted_iota(jnp.int32, (16, 128), 1) // 8
    expand = jnp.where(cell_of == lax.broadcasted_iota(jnp.int32, (16, 128), 0), 1.0, 0.0)
    spread = jnp.dot(
        met_v[...].reshape(24, 16), expand.astype(F32),
        preferred_element_type=F32, precision=lax.Precision.HIGHEST,
    ).reshape(3, 8, 128)
    base = [spread[n] * tab_v[0] for n in range(3)]

    fetch[2].wait()
    for i in range(8):
        for j in range(8):
            m = mob_v[i, :, j, :] * float(WEIGHTS[i] * WEIGHTS[j])
            fx[i, j] = m * base[0]
            fy[i, j] = m * base[1]
            fz[i, j] = m * base[2]
    zz[...] = wide_dot(fz[...].reshape(512, 128), mats[2]).reshape(8, 8, 8, 128)
    squared = DERIV * DERIV
    for j in range(8):
        line = apply_line(squared.T, [fx[i, j] for i in range(8)], 1)
        for i in range(8):
            dg[i, j] = line[i] + zz[i, j]
    for i in range(8):
        line = apply_line(squared.T, [fy[i, j] for j in range(8)], 1)
        for j in range(8):
            dg[i, j] = dg[i, j] + line[j]
    fetch[3].wait()
    sya[0, 0] = load_v[:, 7, 7, :]
    sya[1, 0] = load_v[:, 0, 0, :]
    sya[0, 1] = dg[:, 7, 7, :]
    sya[1, 1] = dg[:, 0, 0, :]

    used = [0]

    def send(src, dst, device):
        n = used[0]
        used[0] += 1
        copy = pltpu.make_async_remote_copy(
            src_ref=src, dst_ref=dst, send_sem=send_sem.at[n], recv_sem=recv_sem.at[n],
            device_id=device, device_id_type=MESH,
        )
        copy.start()
        return copy

    def send_lines(lines, corners, sides):
        return [
            send(lines.at[0], corners.at[0], (dn, sn)),
            send(lines.at[1], corners.at[1], (dn, sp)),
            send(lines.at[0], corners.at[2], (dp, sn)),
            send(lines.at[1], corners.at[3], (dp, sp)),
            send(lines.at[0], sides.at[0], (d, sn)),
            send(lines.at[1], sides.at[1], (d, sp)),
        ]

    pl.semaphore_wait(barrier, 8)
    first = send_lines(sya, rca, rya)
    first += [
        send(dg.at[7], rxd.at[0], (dn, s)),
        send(dg.at[0], rxd.at[1], (dp, s)),
        send(load_hbm.at[0, 7], rxl.at[0], (dn, s)),
        send(load_hbm.at[0, 0], rxl.at[1], (dp, s)),
    ]

    inner = range(1, 7)
    rim = [(i, j) for i in range(8) for j in range(8) if i in (0, 7) or j in (0, 7)]
    deep = [(i, j) for i in inner for j in inner]

    def first_step(i, j, load, diag):
        right = z_joined(load)
        inverse = 1.0 / z_joined(diag)
        rhs[i, j] = right
        dg[i, j] = inverse
        fs[i, j] = inverse * right * float(1.0 / THETA)

    def rim_sums(local, planes, sides, corners):
        out = {}
        rows = {}
        for i in range(8):
            line = {j: local(i, j) for j in (range(8) if i in (0, 7) else (0, 7))}
            if i == 0:
                line = {j: v + planes(0, j) for j, v in line.items()}
            if i == 7:
                line = {j: v + planes(1, j) for j, v in line.items()}
            before, after = sides(0, i), sides(1, i)
            if i == 0:
                before, after = before + corners(0, 7), after + corners(1, 7)
            if i == 7:
                before, after = before + corners(2, 0), after + corners(3, 0)
            low, high = line[0], line[7]
            line[7] = high + jnp.where(sub8 == 7, after, pltpu.roll(low, 7, 0))
            line[0] = low + jnp.where(sub8 == 0, before, pltpu.roll(high, 1, 0))
            for j, v in line.items():
                out[i, j] = v
        return out

    for i, j in deep:
        first_step(i, j, load_v[i, :, j, :], dg[i, j])

    for copy in first:
        copy.wait()
    wide = lambda row: jnp.broadcast_to(row, (8, 128))
    loads = rim_sums(
        lambda i, j: load_v[i, :, j, :],
        lambda side, j: rxl[side, :, j, :],
        lambda side, i: wide(rya[side, 0, i : i + 1, :]),
        lambda slot, i: wide(rca[slot, 0, i : i + 1, :]),
    )
    diags = rim_sums(
        lambda i, j: dg[i, j],
        lambda side, j: rxd[side, j],
        lambda side, i: wide(rya[side, 1, i : i + 1, :]),
        lambda slot, i: wide(rca[slot, 1, i : i + 1, :]),
    )
    for i, j in rim:
        first_step(i, j, loads[i, j], diags[i, j])

    flux = wide_dot(fs[...].reshape(512, 128), mats[0]) * fz[...].reshape(512, 128)
    zz[...] = wide_dot(flux, mats[1]).reshape(8, 8, 8, 128)
    for j in range(8):
        grad = apply_line(DERIV, [fs[i, j] for i in range(8)], -1)
        line = apply_line(DERIV.T, [fx[i, j] * grad[i] for i in range(8)], -1)
        for i in range(8):
            kv[i, j] = line[i] + zz[i, j]
    for i in range(8):
        grad = apply_line(DERIV, [fs[i, j] for j in range(8)], -1)
        line = apply_line(DERIV.T, [fy[i, j] * grad[j] for j in range(8)], -1)
        for j in range(8):
            kv[i, j] = kv[i, j] + line[j]
    syb[0] = kv[:, 7, 7, :]
    syb[1] = kv[:, 0, 0, :]
    second = send_lines(syb, rcb, ryb)
    second += [send(kv.at[7], rxb.at[0], (dn, s)), send(kv.at[0], rxb.at[1], (dp, s))]

    def smoothed(i, j, value):
        resid = rhs[i, j] - z_joined(value)
        p = KEEP * fs[i, j] + STEP * (dg[i, j] * resid)
        pr[i, j] = p
        out_v[i, :, j, :] = p

    for i, j in deep:
        smoothed(i, j, kv[i, j])
    for copy in second:
        copy.wait()
    sums = rim_sums(
        lambda i, j: kv[i, j],
        lambda side, j: rxb[side, j],
        lambda side, i: wide(ryb[side, i : i + 1, :]),
        lambda slot, i: wide(rcb[slot, i : i + 1, :]),
    )
    for i, j in rim:
        smoothed(i, j, sums[i, j])
    write = pltpu.make_async_copy(out_v, press_hbm.at[0], local_sem.at[0])
    write.start()

    def low_high(v):
        plain = total(v)
        slope = total([float(NODES[m]) * (v[m] - v[7 - m]) for m in range(4)])
        return (plain - slope) * 0.125, (plain + slope) * 0.125

    zz[...] = (
        wide_dot(pr[...].reshape(512, 128), mats[0]) * fz[...].reshape(512, 128)
    ).reshape(8, 8, 8, 128)
    along_x = []
    for j in range(8):
        grad = apply_line(DERIV, [pr[i, j] for i in range(8)], -1)
        along_x.append(total([fx[i, j] * grad[i] for i in range(8)]) * 0.125)
    along_y = []
    for i in range(8):
        grad = apply_line(DERIV, [pr[i, j] for j in range(8)], -1)
        along_y.append(total([fy[i, j] * grad[j] for j in range(8)]) * 0.125)
    x_part, y_part = low_high(along_x), low_high(along_y)
    held = [low_high([load_v[i, :, j, :] for i in range(8)]) for j in range(8)]
    flux_z = [low_high([zz[i, j] for i in range(8)]) for j in range(8)]
    plain, cells = [], []
    for p in range(2):
        held_p = low_high([held[j][p] for j in range(8)])
        flux_p = low_high([flux_z[j][p] for j in range(8)])
        for q in range(2):
            x_term = x_part[q] if p else -x_part[q]
            y_term = y_part[p] if q else -y_part[p]
            plain.append(held_p[q] - x_term - y_term)
            cells.append(-flux_p[q])
    vertex = wide_dot(jnp.concatenate(plain, axis=0), mats[3]) + wide_dot(
        jnp.concatenate(cells, axis=0), mats[4]
    )
    corner = [[vertex[16 * p + 8 * q : 16 * p + 8 * q + 8] for q in range(2)] for p in range(2)]
    row = []
    for p in range(2):
        moved = pltpu.roll(corner[p][1], 1, 0)
        row.append(corner[p][0] + jnp.where(sub8 == 0, 0.0, moved))
        sc[1 + p] = jnp.where(sub8 == 0, moved, 0.0)
    sc[0] = row[1]
    third = [
        send(sc.at[2], rc.at[2], (dn, sn)),
        send(sc.at[0], rc.at[0], (dn, s)),
        send(sc.at[1], rc.at[1], (d, sn)),
    ]
    for copy in third:
        copy.wait()
    coarse = row[0] + rc[0] + (rc[1] + rc[2])
    coarse_ref[0] = coarse[:, 0:17]
    write.wait()


def shards(element_load, mobility, metric):
    field = pltpu.VMEM((8, 8, 8, 128), F32)
    hbm = pl.BlockSpec(memory_space=pltpu.HBM)
    return pl.pallas_call(
        kernel,
        name="smoother",
        out_shape=(
            jax.ShapeDtypeStruct((1, 8, 8, 8, 128), F32),
            jax.ShapeDtypeStruct((1, 8, 17), F32),
        ),
        in_specs=[hbm, hbm, hbm, hbm],
        out_specs=(hbm, pl.BlockSpec(memory_space=pltpu.VMEM)),
        scratch_shapes=[
            field, field,
            pltpu.VMEM((3, 1, 8, 16), F32),
            pltpu.VMEM((5, 8, 128), F32),
            pltpu.VMEM((5, 256, 256), BF16),
            field, field, field, field, field, field, field, field, field, field,
            pltpu.VMEM((2, 2, 8, 128), F32),
            pltpu.VMEM((2, 8, 128), F32),
            pltpu.VMEM((3, 8, 128), F32),
            pltpu.VMEM((2, 8, 8, 128), F32),
            pltpu.VMEM((2, 8, 8, 128), F32),
            pltpu.VMEM((2, 2, 8, 128), F32),
            pltpu.VMEM((4, 2, 8, 128), F32),
            pltpu.VMEM((2, 8, 8, 128), F32),
            pltpu.VMEM((2, 8, 128), F32),
            pltpu.VMEM((4, 8, 128), F32),
            pltpu.VMEM((3, 8, 128), F32),
            pltpu.SemaphoreType.DMA((4,)),
            pltpu.SemaphoreType.DMA((21,)),
            pltpu.SemaphoreType.DMA((21,)),
        ],
        compiler_params=pltpu.CompilerParams(collective_id=0, has_side_effects=True),
    )(element_load, mobility, metric, jnp.asarray(small_tables()))


def solution(mesh):
    in_specs = (
        P("dom", None, "sub", None, None),
        P("dom", None, "sub", None, None),
        P(None, "dom", "sub", None),
    )
    out_specs = (P("dom", None, "sub", None, None), P("dom", "sub", None))
    return jax.shard_map(shards, mesh=mesh, in_specs=in_specs, out_specs=out_specs, check_vma=False)
```

time: 98.4 us -> 41.3 us (0.42)
  the two profiles are of different devices: /device:TPU:24 before, /device:TPU:1 now
where the time goes in v1:
time: 41.3 us; the launch traced here: 41.1 us
  Pallas kernels  38.2 us (92%)
  local copies, waits for them, and re-layouts  2.27 us (5%)
  between operations  0.65 us (2%)
    pallas_call x1, Pallas kernels, shards(): pl.pallas_call(kernel, name='smoother', out_shape=(jax.ShapeDtypeStruct((...  38.2 us
    unnamed x4, local copies, waits for them, and re-layouts  2.27 us

profile of v1, /device:TPU:1, one launch (start us, length us, event | category | flops | bytes accessed | tf_op | source)
XLA Modules:
  0.0 41.1 jit_solution(14685709124729847184)
XLA Ops:
  0.6 38.2 %smoother.1 = (f32[1,8,8,8,128]{4,3,2,1,0:T(8,128)}, f32[1,8,17]{2,1,0:T(8,128)}) custom-call(f32[1,8,8,8,128]{4,3,2,1,0:T(8,128)} %load_hbm.1, f32[1,8,8,8,128]{4,3,2,1,0:T(8,128)} %mob_hbm.1, f32[3,1,8,16]{3,2,1,0:T(8,128)} %met_hbm.1, f32[5,8,128]{2,1,0:T(8,128)} %constant.2.clone.tab_hbm), custom_call_target="tpu_custom_call" | custom-call | tf_op jit(solution)/shard_map/smoother/pallas_call | solution.py:369
  38.8 0.0 copy-start
  38.8 1.7 %copy.8 = f32[1,8,8,8,128]{4,3,2,1,0:T(8,128)} copy(f32[1,8,8,8,128]{4,3,2,1,0:T(8,128)} %get-tuple-element.4) | data formatting | bytes 524288
  40.5 0.0 copy-done
  40.5 0.6 %copy.9 = f32[1,8,17]{2,1,0:T(8,128)} copy(f32[1,8,17]{2,1,0:T(8,128)S(1)} %copy-done) | data formatting | bytes 1088
Async XLA Ops:
  38.8 1.7 %copy-start = (f32[1,8,17]{2,1,0:T(8,128)S(1)}, f32[1,8,17]{2,1,0:T(8,128)}, u32[]{:S(2)}) copy-start(f32[1,8,17]{2,1,0:T(8,128)} %get-tuple-element.5) | copy-start | bytes 1636

commit v2 on v1

--- a/solution.py
+++ b/solution.py
@@ -103,11 +103,11 @@
 
 def kernel(
     load_hbm, mob_hbm, met_hbm, tab_hbm,
-    press_hbm, coarse_ref,
+    press_ref, coarse_ref,
     load_v, mob_v, met_v, tab_v, mats,
-    fx, fy, fz, dg, rhs, fs, kv, zz, pr, out_v,
-    sya, syb, sc,
-    rxl, rxd, rya, rca, rxb, ryb, rcb, rc,
+    fx, fy, fz, dg, inv, rhs, fs, kv, zz, gx, gy, gz,
+    hold, sya, sg, syb, sc,
+    rxl, rxd, rxg, rya, rca, rxb, ryb, rcb, rc,
     local_sem, send_sem, recv_sem,
 ):
     d, s = lax.axis_index("dom"), lax.axis_index("sub")
@@ -230,22 +230,19 @@
         right = z_joined(load)
         inverse = 1.0 / z_joined(diag)
         rhs[i, j] = right
-        dg[i, j] = inverse
+        inv[i, j] = inverse
         fs[i, j] = inverse * right * float(1.0 / THETA)
 
-    def rim_sums(local, planes, sides, corners):
+    def rim_sums(planes_i, local, planes, sides, corners):
         out = {}
-        rows = {}
-        for i in range(8):
+        for i in planes_i:
             line = {j: local(i, j) for j in (range(8) if i in (0, 7) else (0, 7))}
+            before, after = sides(0, i), sides(1, i)
             if i == 0:
                 line = {j: v + planes(0, j) for j, v in line.items()}
+                before, after = before + corners(0, 7), after + corners(1, 7)
             if i == 7:
                 line = {j: v + planes(1, j) for j, v in line.items()}
-            before, after = sides(0, i), sides(1, i)
-            if i == 0:
-                before, after = before + corners(0, 7), after + corners(1, 7)
-            if i == 7:
                 before, after = before + corners(2, 0), after + corners(3, 0)
             low, high = line[0], line[7]
             line[7] = high + jnp.where(sub8 == 7, after, pltpu.roll(low, 7, 0))
@@ -254,19 +251,48 @@
                 out[i, j] = v
         return out
 
+    gz[...] = wide_dot(fz[...].reshape(512, 128), mats[1]).reshape(8, 8, 8, 128)
+    for j in range(8):
+        line = apply_line(DERIV.T / 8.0, [fx[i, j] for i in range(8)], -1)
+        for i in range(8):
+            gx[i, j] = line[i]
+        sg[0, j] = line[7]
+    for i in range(8):
+        line = apply_line(DERIV.T / 8.0, [fy[i, j] for j in range(8)], -1)
+        for j in range(8):
+            gy[i, j] = line[j]
+            if i == 7:
+                sg[1, j] = line[j]
+    for j in range(8):
+        sg[2, j] = gz[7, j]
+    first.append(send(sg, rxg, (dn, s)))
+
     for i, j in deep:
         first_step(i, j, load_v[i, :, j, :], dg[i, j])
 
-    for copy in first:
-        copy.wait()
+    def low_high(v):
+        plain = total(v)
+        slope = total([float(NODES[m]) * (v[m] - v[7 - m]) for m in range(4)])
+        return (plain - slope) * 0.125, (plain + slope) * 0.125
+
+    held = [low_high([load_v[i, :, j, :] for i in range(8)]) for j in range(8)]
+    held = [low_high([held[j][p] for j in range(8)]) for p in range(2)]
+    for p in range(2):
+        for q in range(2):
+            hold[2 * p + q] = held[p][q]
+
+    for copy in first[:10]:
+        copy.wait_recv()
     wide = lambda row: jnp.broadcast_to(row, (8, 128))
     loads = rim_sums(
+        range(8),
         lambda i, j: load_v[i, :, j, :],
         lambda side, j: rxl[side, :, j, :],
         lambda side, i: wide(rya[side, 0, i : i + 1, :]),
         lambda slot, i: wide(rca[slot, 0, i : i + 1, :]),
     )
     diags = rim_sums(
+        range(8),
         lambda i, j: dg[i, j],
         lambda side, j: rxd[side, j],
         lambda side, i: wide(rya[side, 1, i : i + 1, :]),
@@ -292,100 +318,116 @@
     second = send_lines(syb, rcb, ryb)
     second += [send(kv.at[7], rxb.at[0], (dn, s)), send(kv.at[0], rxb.at[1], (dp, s))]
 
+    weight = [[float((1.0 + (2 * p - 1) * NODES[m]) / 8.0) for m in range(8)] for p in range(2)]
+    part_x, part_y, part_z = [[] for _ in range(8)], [[] for _ in range(8)], {}
+
     def smoothed(i, j, value):
         resid = rhs[i, j] - z_joined(value)
-        p = KEEP * fs[i, j] + STEP * (dg[i, j] * resid)
-        pr[i, j] = p
-        out_v[i, :, j, :] = p
+        p = KEEP * fs[i, j] + STEP * (inv[i, j] * resid)
+        fs[i, j] = p
+        press_ref[0, i, :, j, :] = p
 
     for i, j in deep:
         smoothed(i, j, kv[i, j])
-    for copy in second:
-        copy.wait()
-    sums = rim_sums(
-        lambda i, j: kv[i, j],
-        lambda side, j: rxb[side, j],
-        lambda side, i: wide(ryb[side, i : i + 1, :]),
-        lambda slot, i: wide(rcb[slot, i : i + 1, :]),
-    )
-    for i, j in rim:
-        smoothed(i, j, sums[i, j])
-    write = pltpu.make_async_copy(out_v, press_hbm.at[0], local_sem.at[0])
-    write.start()
-
-    def low_high(v):
-        plain = total(v)
-        slope = total([float(NODES[m]) * (v[m] - v[7 - m]) for m in range(4)])
-        return (plain - slope) * 0.125, (plain + slope) * 0.125
-
-    zz[...] = (
-        wide_dot(pr[...].reshape(512, 128), mats[0]) * fz[...].reshape(512, 128)
-    ).reshape(8, 8, 8, 128)
-    along_x = []
-    for j in range(8):
-        grad = apply_line(DERIV, [pr[i, j] for i in range(8)], -1)
-        along_x.append(total([fx[i, j] * grad[i] for i in range(8)]) * 0.125)
-    along_y = []
-    for i in range(8):
-        grad = apply_line(DERIV, [pr[i, j] for j in range(8)], -1)
-        along_y.append(total([fy[i, j] * grad[j] for j in range(8)]) * 0.125)
-    x_part, y_part = low_high(along_x), low_high(along_y)
-    held = [low_high([load_v[i, :, j, :] for i in range(8)]) for j in range(8)]
-    flux_z = [low_high([zz[i, j] for i in range(8)]) for j in range(8)]
-    plain, cells = [], []
-    for p in range(2):
-        held_p = low_high([held[j][p] for j in range(8)])
-        flux_p = low_high([flux_z[j][p] for j in range(8)])
-        for q in range(2):
-            x_term = x_part[q] if p else -x_part[q]
-            y_term = y_part[p] if q else -y_part[p]
-            plain.append(held_p[q] - x_term - y_term)
-            cells.append(-flux_p[q])
-    vertex = wide_dot(jnp.concatenate(plain, axis=0), mats[3]) + wide_dot(
-        jnp.concatenate(cells, axis=0), mats[4]
-    )
-    corner = [[vertex[16 * p + 8 * q : 16 * p + 8 * q + 8] for q in range(2)] for p in range(2)]
-    row = []
-    for p in range(2):
-        moved = pltpu.roll(corner[p][1], 1, 0)
-        row.append(corner[p][0] + jnp.where(sub8 == 0, 0.0, moved))
-        sc[1 + p] = jnp.where(sub8 == 0, moved, 0.0)
-    sc[0] = row[1]
+
+    def finish(planes_i):
+        sums = rim_sums(
+            planes_i,
+            lambda i, j: kv[i, j],
+            lambda side, j: rxb[side, j],
+            lambda side, i: wide(ryb[side, i : i + 1, :]),
+            lambda slot, i: wide(rcb[slot, i : i + 1, :]),
+        )
+        for (i, j), value in sums.items():
+            smoothed(i, j, value)
+
+    def weigh(line, p):
+        return total([weight[p][m] * v for m, v in enumerate(line) if weight[p][m] != 0.0])
+
+    def vertices(plain, cells):
+        both = wide_dot(jnp.concatenate(plain, axis=0), mats[3]) + wide_dot(
+            jnp.concatenate(cells, axis=0), mats[4]
+        )
+        inside, edge = both[0:8], pltpu.roll(both[8:16], 1, 0)
+        return inside + jnp.where(sub8 == 0, 0.0, edge), jnp.where(sub8 == 0, edge, 0.0)
+
+    for n in (4, 5):
+        second[n].wait_recv()
+    finish(inner)
+    for n in (0, 1, 6):
+        second[n].wait_recv()
+    finish((0,))
+    x_sum = [total([gx[i, j] * fs[i, j] for i in range(7)]) for j in range(8)]
+    y_sum = [total([gy[i, j] * fs[i, j] for j in range(8)]) for i in range(7)]
+    z_line = []
+    for i in range(7):
+        terms = [gz[i, j] * fs[i, j] for j in range(8)]
+        z_line.append([weigh(terms, q) for q in range(2)])
+    y_high = weigh(y_sum, 1)
+    plain = [
+        hold[2] - weigh(x_sum, 0) + y_high,
+        hold[3] - weigh(x_sum, 1) - y_high,
+    ]
+    cells = [-weigh([z[q] for z in z_line], 1) for q in range(2)]
+    sc[0], sc[1] = vertices(plain, cells)
     third = [
-        send(sc.at[2], rc.at[2], (dn, sn)),
+        send(sc.at[1], rc.at[1], (dn, sn)),
         send(sc.at[0], rc.at[0], (dn, s)),
-        send(sc.at[1], rc.at[1], (d, sn)),
-    ]
+    ]
+    for n in (2, 3, 7):
+        second[n].wait_recv()
+    finish((7,))
+    first[10].wait_recv()
+    x_sum = [x_sum[j] + gx[7, j] * fs[7, j] for j in range(8)]
+    y_low = weigh(y_sum + [y_sum[0]], 0)
+    x_net = [x_sum[j] - rxg[0, j] * fs[0, j] for j in range(8)]
+    y_face = 0.25 * total([rxg[1, j] * fs[0, j] for j in range(8)])
+    z_face = [rxg[2, j] * fs[0, j] for j in range(8)]
+    plain = [
+        hold[0] + weigh(x_net, 0) + (y_low + y_face),
+        hold[1] + weigh(x_net, 1) - (y_low + y_face),
+    ]
+    cells = [
+        -weigh([z[q] for z in z_line] + [z_line[0][q]], 0) - 0.25 * weigh(z_face, q)
+        for q in range(2)
+    ]
+    own, sc[2] = vertices(plain, cells)
+    third.append(send(sc.at[2], rc.at[2], (d, sn)))
     for copy in third:
-        copy.wait()
-    coarse = row[0] + rc[0] + (rc[1] + rc[2])
+        copy.wait_recv()
+    coarse = own + rc[0] + (rc[1] + rc[2])
     coarse_ref[0] = coarse[:, 0:17]
-    write.wait()
+    for copy in first + second + third:
+        copy.wait_send()
 
 
 def shards(element_load, mobility, metric):
     field = pltpu.VMEM((8, 8, 8, 128), F32)
     hbm = pl.BlockSpec(memory_space=pltpu.HBM)
+    vmem = pl.BlockSpec(memory_space=pltpu.VMEM)
     return pl.pallas_call(
         kernel,
         name="smoother",
         out_shape=(
-            jax.ShapeDtypeStruct((1, 8, 8, 8, 128), F32),
-            jax.ShapeDtypeStruct((1, 8, 17), F32),
+            pltpu.VMEM((1, 8, 8, 8, 128), F32),
+            pltpu.VMEM((1, 8, 17), F32),
         ),
         in_specs=[hbm, hbm, hbm, hbm],
-        out_specs=(hbm, pl.BlockSpec(memory_space=pltpu.VMEM)),
+        out_specs=(vmem, vmem),
         scratch_shapes=[
             field, field,
             pltpu.VMEM((3, 1, 8, 16), F32),
             pltpu.VMEM((5, 8, 128), F32),
             pltpu.VMEM((5, 256, 256), BF16),
-            field, field, field, field, field, field, field, field, field, field,
+            *[field] * 12,
+            pltpu.VMEM((4, 8, 128), F32),
             pltpu.VMEM((2, 2, 8, 128), F32),
+            pltpu.VMEM((3, 8, 8, 128), F32),
             pltpu.VMEM((2, 8, 128), F32),
             pltpu.VMEM((3, 8, 128), F32),
             pltpu.VMEM((2, 8, 8, 128), F32),
             pltpu.VMEM((2, 8, 8, 128), F32),
+            pltpu.VMEM((3, 8, 8, 128), F32),
             pltpu.VMEM((2, 2, 8, 128), F32),
             pltpu.VMEM((4, 2, 8, 128), F32),
             pltpu.VMEM((2, 8, 8, 128), F32),
@@ -393,8 +435,8 @@
             pltpu.VMEM((4, 8, 128), F32),
             pltpu.VMEM((3, 8, 128), F32),
             pltpu.SemaphoreType.DMA((4,)),
-            pltpu.SemaphoreType.DMA((21,)),
-            pltpu.SemaphoreType.DMA((21,)),
+            pltpu.SemaphoreType.DMA((22,)),
+            pltpu.SemaphoreType.DMA((22,)),
         ],
         compiler_params=pltpu.CompilerParams(collective_id=0, has_side_effects=True),
     )(element_load, mobility, metric, jnp.asarray(small_tables()))

time: 41.3 us -> 38.7 us (0.937)
  Pallas kernels: 38.2 us -> 36.6 us
  local copies, waits for them, and re-layouts: 2.27 us -> 1.3 us
    pallas_call x1, Pallas kernels: 38.2 us -> 36.6 us  [shards(): pl.pallas_call(kernel, name='smoother', out_shape=(pltpu.VMEM((1, 8, 8, 8...]
    unnamed x4 -> x2, local copies, waits for them, and re-layouts: 2.27 us -> 1.3 us
where the time goes in v2:
time: 38.7 us; the launch traced here: 38.5 us
  Pallas kernels  36.6 us (95%)
  local copies, waits for them, and re-layouts  1.3 us (3%)
  between operations  0.64 us (2%)
    pallas_call x1, Pallas kernels, shards(): pl.pallas_call(kernel, name='smoother', out_shape=(pltpu.VMEM((1, 8, 8, 8...  36.6 us
    unnamed x2, local copies, waits for them, and re-layouts  1.3 us

profile of v2, /device:TPU:1, one launch (start us, length us, event | category | flops | bytes accessed | tf_op | source)
XLA Modules:
  0.0 38.5 jit_solution(12578040678999511702)
XLA Ops:
  0.6 36.6 %smoother.1 = (f32[1,8,8,8,128]{4,3,2,1,0:T(8,128)S(1)}, f32[1,8,17]{2,1,0:T(8,128)S(1)}) custom-call(f32[1,8,8,8,128]{4,3,2,1,0:T(8,128)} %load_hbm.1, f32[1,8,8,8,128]{4,3,2,1,0:T(8,128)} %mob_hbm.1, f32[3,1,8,16]{3,2,1,0:T(8,128)} %met_hbm.1, f32[5,8,128]{2,1,0:T(8,128)} %constant.2.clone.tab_hbm), custom_call_target="tpu_custom_call" | custom-call | tf_op jit(solution)/shard_map/smoother/pallas_call | solution.py:408
  37.2 0.7 %copy.8 = f32[1,8,8,8,128]{4,3,2,1,0:T(8,128)} copy(f32[1,8,8,8,128]{4,3,2,1,0:T(8,128)S(1)} %get-tuple-element.2) | data formatting | bytes 524288
  37.9 0.6 %copy.9 = f32[1,8,17]{2,1,0:T(8,128)} copy(f32[1,8,17]{2,1,0:T(8,128)S(1)} %get-tuple-element.3) | data formatting | bytes 1088

commit v3 on v2

--- a/solution.py
+++ b/solution.py
@@ -76,8 +76,9 @@
 
 
 def apply_line(matrix, v, sign):
-    even = [v[m] + v[7 - m] for m in range(4)]
-    odd = [v[m] - v[7 - m] for m in range(4)]
+    pair = [(v[m], v[7 - m]) for m in range(4)]
+    even = [x if y is None else x + y for x, y in pair]
+    odd = [x if y is None else x - y for x, y in pair]
     out = [None] * 8
     for a in range(4):
         with_even = total(
@@ -105,9 +106,9 @@
     load_hbm, mob_hbm, met_hbm, tab_hbm,
     press_ref, coarse_ref,
     load_v, mob_v, met_v, tab_v, mats,
-    fx, fy, fz, dg, inv, rhs, fs, kv, zz, gx, gy, gz,
-    hold, sya, sg, syb, sc,
-    rxl, rxd, rxg, rya, rca, rxb, ryb, rcb, rc,
+    fx, fy, fz, dg, inv, rhs, fs, kv, zz, gx, gy, gz, k7,
+    hold, sya, sg, sgx, sk, syb, sye, syc, sc,
+    rxl, rxd, rxg, rxgx, rya, rca, rk, rxb, ryb, rcb, rc,
     local_sem, send_sem, recv_sem,
 ):
     d, s = lax.axis_index("dom"), lax.axis_index("sub")
@@ -175,12 +176,17 @@
             fx[i, j] = m * base[0]
             fy[i, j] = m * base[1]
             fz[i, j] = m * base[2]
+            if i == 7:
+                sg[j] = m
+    sg[8] = base[1]
+    sg[9] = base[2]
     zz[...] = wide_dot(fz[...].reshape(512, 128), mats[2]).reshape(8, 8, 8, 128)
     squared = DERIV * DERIV
     for j in range(8):
         line = apply_line(squared.T, [fx[i, j] for i in range(8)], 1)
         for i in range(8):
             dg[i, j] = line[i] + zz[i, j]
+        sg[10 + j] = line[7]
     for i in range(8):
         line = apply_line(squared.T, [fy[i, j] for j in range(8)], 1)
         for j in range(8):
@@ -203,23 +209,19 @@
         copy.start()
         return copy
 
-    def send_lines(lines, corners, sides):
-        return [
-            send(lines.at[0], corners.at[0], (dn, sn)),
-            send(lines.at[1], corners.at[1], (dn, sp)),
-            send(lines.at[0], corners.at[2], (dp, sn)),
-            send(lines.at[1], corners.at[3], (dp, sp)),
-            send(lines.at[0], sides.at[0], (d, sn)),
-            send(lines.at[1], sides.at[1], (d, sp)),
-        ]
-
     pl.semaphore_wait(barrier, 8)
-    first = send_lines(sya, rca, rya)
-    first += [
+    first = [
+        send(sya.at[0], rca.at[0], (dn, sn)),
+        send(sya.at[1], rca.at[1], (dn, sp)),
+        send(sya.at[0], rca.at[2], (dp, sn)),
+        send(sya.at[1], rca.at[3], (dp, sp)),
+        send(sya.at[0], rya.at[0], (d, sn)),
+        send(sya.at[1], rya.at[1], (d, sp)),
         send(dg.at[7], rxd.at[0], (dn, s)),
         send(dg.at[0], rxd.at[1], (dp, s)),
         send(load_hbm.at[0, 7], rxl.at[0], (dn, s)),
         send(load_hbm.at[0, 0], rxl.at[1], (dp, s)),
+        send(sg, rxg, (dn, s)),
     ]
 
     inner = range(1, 7)
@@ -251,21 +253,27 @@
                 out[i, j] = v
         return out
 
-    gz[...] = wide_dot(fz[...].reshape(512, 128), mats[1]).reshape(8, 8, 8, 128)
     for j in range(8):
-        line = apply_line(DERIV.T / 8.0, [fx[i, j] for i in range(8)], -1)
+        line = [fx[a, j] for a in range(8)]
+        for i in range(7):
+            k7[i, j] = total([float(DERIV[a, i] * DERIV[a, 7]) * line[a] for a in range(8)])
+        line = apply_line(DERIV.T / 8.0, line, -1)
         for i in range(8):
             gx[i, j] = line[i]
-        sg[0, j] = line[7]
-    for i in range(8):
+        sgx[j] = line[7]
+        k7[7, j] = jnp.zeros((8, 128), F32)
+    sk[0] = k7[:, 7, 7, :]
+    sk[1] = k7[:, 0, 0, :]
+    first += [
+        send(sk.at[0], rk.at[0], (d, sn)),
+        send(sk.at[1], rk.at[1], (d, sp)),
+        send(sgx, rxgx, (dn, s)),
+    ]
+    gz[1:7] = wide_dot(fz[1:7].reshape(384, 128), mats[1]).reshape(6, 8, 8, 128)
+    for i in range(1, 7):
         line = apply_line(DERIV.T / 8.0, [fy[i, j] for j in range(8)], -1)
         for j in range(8):
             gy[i, j] = line[j]
-            if i == 7:
-                sg[1, j] = line[j]
-    for j in range(8):
-        sg[2, j] = gz[7, j]
-    first.append(send(sg, rxg, (dn, s)))
 
     for i, j in deep:
         first_step(i, j, load_v[i, :, j, :], dg[i, j])
@@ -281,42 +289,87 @@
         for q in range(2):
             hold[2 * p + q] = held[p][q]
 
-    for copy in first[:10]:
-        copy.wait_recv()
     wide = lambda row: jnp.broadcast_to(row, (8, 128))
-    loads = rim_sums(
-        range(8),
-        lambda i, j: load_v[i, :, j, :],
-        lambda side, j: rxl[side, :, j, :],
-        lambda side, i: wide(rya[side, 0, i : i + 1, :]),
-        lambda slot, i: wide(rca[slot, 0, i : i + 1, :]),
-    )
-    diags = rim_sums(
-        range(8),
-        lambda i, j: dg[i, j],
-        lambda side, j: rxd[side, j],
-        lambda side, i: wide(rya[side, 1, i : i + 1, :]),
-        lambda slot, i: wide(rca[slot, 1, i : i + 1, :]),
-    )
-    for i, j in rim:
-        first_step(i, j, loads[i, j], diags[i, j])
-
-    flux = wide_dot(fs[...].reshape(512, 128), mats[0]) * fz[...].reshape(512, 128)
-    zz[...] = wide_dot(flux, mats[1]).reshape(8, 8, 8, 128)
+
+    def start_rim(planes_i):
+        loads = rim_sums(
+            planes_i,
+            lambda i, j: load_v[i, :, j, :],
+            lambda side, j: rxl[side, :, j, :],
+            lambda side, i: wide(rya[side, 0, i : i + 1, :]),
+            lambda slot, i: wide(rca[slot, 0, i : i + 1, :]),
+        )
+        diags = rim_sums(
+            planes_i,
+            lambda i, j: dg[i, j],
+            lambda side, j: rxd[side, j],
+            lambda side, i: wide(rya[side, 1, i : i + 1, :]),
+            lambda slot, i: wide(rca[slot, 1, i : i + 1, :]),
+        )
+        for i, j in loads:
+            first_step(i, j, loads[i, j], diags[i, j])
+
+    for n in (4, 5):
+        first[n].wait_recv()
+    start_rim(inner)
+    for n in (0, 1, 6, 8):
+        first[n].wait_recv()
+    start_rim((0,))
     for j in range(8):
-        grad = apply_line(DERIV, [fs[i, j] for i in range(8)], -1)
+        grad = apply_line(DERIV, [fs[i, j] for i in range(7)] + [None], -1)
         line = apply_line(DERIV.T, [fx[i, j] * grad[i] for i in range(8)], -1)
         for i in range(8):
-            kv[i, j] = line[i] + zz[i, j]
-    for i in range(8):
-        grad = apply_line(DERIV, [fs[i, j] for j in range(8)], -1)
-        line = apply_line(DERIV.T, [fy[i, j] * grad[j] for j in range(8)], -1)
-        for j in range(8):
-            kv[i, j] = kv[i, j] + line[j]
+            kv[i, j] = line[i]
+    sye[0] = kv[:, 7, 7, :]
+    sye[1] = kv[:, 0, 0, :]
+    second = [
+        send(sye.at[0], rcb.at[0], (dn, sn)),
+        send(sye.at[1], rcb.at[1], (dn, sp)),
+        send(kv.at[7], rxb.at[0], (dn, s)),
+    ]
+
+    def yz_part(low, high):
+        rows = 64 * (high - low)
+        flux = wide_dot(fs[low:high].reshape(rows, 128), mats[0]) * fz[low:high].reshape(rows, 128)
+        zz[low:high] = wide_dot(flux, mats[1]).reshape(high - low, 8, 8, 128)
+        for i in range(low, high):
+            grad = apply_line(DERIV, [fs[i, j] for j in range(8)], -1)
+            line = apply_line(DERIV.T, [fy[i, j] * grad[j] for j in range(8)], -1)
+            for j in range(8):
+                kv[i, j] = kv[i, j] + (line[j] + zz[i, j])
+
+    yz_part(1, 7)
+    first[10].wait_recv()
+    for j in range(8):
+        fy[0, j] = fy[0, j] + rxg[j] * rxg[8]
+        fz[0, j] = fz[0, j] + rxg[j] * rxg[9]
+        kv[0, j] = kv[0, j] + rxg[10 + j] * fs[0, j]
+    yz_part(0, 1)
     syb[0] = kv[:, 7, 7, :]
     syb[1] = kv[:, 0, 0, :]
-    second = send_lines(syb, rcb, ryb)
-    second += [send(kv.at[7], rxb.at[0], (dn, s)), send(kv.at[0], rxb.at[1], (dp, s))]
+    second += [send(syb.at[0], ryb.at[0], (d, sn)), send(syb.at[1], ryb.at[1], (d, sp))]
+
+    for n in (2, 3, 7, 9):
+        first[n].wait_recv()
+    start_rim((7,))
+    for j in range(8):
+        v = fs[7, j]
+        for i in range(7):
+            kv[i, j] = kv[i, j] + k7[i, j] * v
+    syc[0] = kv[:, 7, 7, :]
+    syc[1] = kv[:, 0, 0, :]
+    second += [
+        send(syc.at[0], rcb.at[2], (dp, sn)),
+        send(syc.at[1], rcb.at[3], (dp, sp)),
+        send(kv.at[0], rxb.at[1], (dp, s)),
+    ]
+    gz[0] = wide_dot(fz[0].reshape(64, 128), mats[1]).reshape(8, 8, 128)
+    line = apply_line(DERIV.T / 8.0, [fy[0, j] for j in range(8)], -1)
+    for j in range(8):
+        gy[0, j] = line[j]
+    for n in (11, 12):
+        first[n].wait_recv()
+    ends = [fs[7, 0], fs[7, 7]]
 
     weight = [[float((1.0 + (2 * p - 1) * NODES[m]) / 8.0) for m in range(8)] for p in range(2)]
     part_x, part_y, part_z = [[] for _ in range(8)], [[] for _ in range(8)], {}
@@ -335,7 +388,8 @@
             planes_i,
             lambda i, j: kv[i, j],
             lambda side, j: rxb[side, j],
-            lambda side, i: wide(ryb[side, i : i + 1, :]),
+            lambda side, i: wide(ryb[side, i : i + 1, :])
+            + (wide(rk[side, i : i + 1, :]) * ends[side] if i < 7 else 0.0),
             lambda slot, i: wide(rcb[slot, i : i + 1, :]),
         )
         for (i, j), value in sums.items():
@@ -351,10 +405,10 @@
         inside, edge = both[0:8], pltpu.roll(both[8:16], 1, 0)
         return inside + jnp.where(sub8 == 0, 0.0, edge), jnp.where(sub8 == 0, edge, 0.0)
 
-    for n in (4, 5):
+    for n in (3, 4):
         second[n].wait_recv()
     finish(inner)
-    for n in (0, 1, 6):
+    for n in (0, 1, 2):
         second[n].wait_recv()
     finish((0,))
     x_sum = [total([gx[i, j] * fs[i, j] for i in range(7)]) for j in range(8)]
@@ -374,23 +428,17 @@
         send(sc.at[1], rc.at[1], (dn, sn)),
         send(sc.at[0], rc.at[0], (dn, s)),
     ]
-    for n in (2, 3, 7):
+    for n in (5, 6, 7):
         second[n].wait_recv()
     finish((7,))
-    first[10].wait_recv()
-    x_sum = [x_sum[j] + gx[7, j] * fs[7, j] for j in range(8)]
+    first[13].wait_recv()
+    x_net = [x_sum[j] + gx[7, j] * fs[7, j] - rxgx[j] * fs[0, j] for j in range(8)]
     y_low = weigh(y_sum + [y_sum[0]], 0)
-    x_net = [x_sum[j] - rxg[0, j] * fs[0, j] for j in range(8)]
-    y_face = 0.25 * total([rxg[1, j] * fs[0, j] for j in range(8)])
-    z_face = [rxg[2, j] * fs[0, j] for j in range(8)]
     plain = [
-        hold[0] + weigh(x_net, 0) + (y_low + y_face),
-        hold[1] + weigh(x_net, 1) - (y_low + y_face),
-    ]
-    cells = [
-        -weigh([z[q] for z in z_line] + [z_line[0][q]], 0) - 0.25 * weigh(z_face, q)
-        for q in range(2)
-    ]
+        hold[0] + weigh(x_net, 0) + y_low,
+        hold[1] + weigh(x_net, 1) - y_low,
+    ]
+    cells = [-weigh([z[q] for z in z_line] + [z_line[0][q]], 0) for q in range(2)]
     own, sc[2] = vertices(plain, cells)
     third.append(send(sc.at[2], rc.at[2], (d, sn)))
     for copy in third:
@@ -419,24 +467,30 @@
             pltpu.VMEM((3, 1, 8, 16), F32),
             pltpu.VMEM((5, 8, 128), F32),
             pltpu.VMEM((5, 256, 256), BF16),
-            *[field] * 12,
+            *[field] * 13,
             pltpu.VMEM((4, 8, 128), F32),
             pltpu.VMEM((2, 2, 8, 128), F32),
-            pltpu.VMEM((3, 8, 8, 128), F32),
+            pltpu.VMEM((18, 8, 128), F32),
+            pltpu.VMEM((8, 8, 128), F32),
+            pltpu.VMEM((2, 8, 128), F32),
+            pltpu.VMEM((2, 8, 128), F32),
+            pltpu.VMEM((2, 8, 128), F32),
             pltpu.VMEM((2, 8, 128), F32),
             pltpu.VMEM((3, 8, 128), F32),
             pltpu.VMEM((2, 8, 8, 128), F32),
             pltpu.VMEM((2, 8, 8, 128), F32),
-            pltpu.VMEM((3, 8, 8, 128), F32),
+            pltpu.VMEM((18, 8, 128), F32),
+            pltpu.VMEM((8, 8, 128), F32),
             pltpu.VMEM((2, 2, 8, 128), F32),
             pltpu.VMEM((4, 2, 8, 128), F32),
+            pltpu.VMEM((2, 8, 128), F32),
             pltpu.VMEM((2, 8, 8, 128), F32),
             pltpu.VMEM((2, 8, 128), F32),
             pltpu.VMEM((4, 8, 128), F32),
             pltpu.VMEM((3, 8, 128), F32),
             pltpu.SemaphoreType.DMA((4,)),
-            pltpu.SemaphoreType.DMA((22,)),
-            pltpu.SemaphoreType.DMA((22,)),
+            pltpu.SemaphoreType.DMA((25,)),
+            pltpu.SemaphoreType.DMA((25,)),
         ],
         compiler_params=pltpu.CompilerParams(collective_id=0, has_side_effects=True),
     )(element_load, mobility, metric, jnp.asarray(small_tables()))

time: 38.7 us -> 36.2 us (0.935)
  Pallas kernels: 36.6 us -> 34.1 us
    pallas_call x1, Pallas kernels: 36.6 us -> 34.1 us  [shards(): pl.pallas_call(kernel, name='smoother', out_shape=(pltpu.VMEM((1, 8, 8, 8...]
where the time goes in v3:
time: 36.2 us; the launch traced here: 36 us
  Pallas kernels  34.1 us (94%)
  local copies, waits for them, and re-layouts  1.3 us (4%)
  between operations  0.64 us (2%)
    pallas_call x1, Pallas kernels, shards(): pl.pallas_call(kernel, name='smoother', out_shape=(pltpu.VMEM((1, 8, 8, 8...  34.1 us
    unnamed x2, local copies, waits for them, and re-layouts  1.3 us

profile of v3, /device:TPU:1, one launch (start us, length us, event | category | flops | bytes accessed | tf_op | source)
XLA Modules:
  0.0 36.0 jit_solution(14000347575435038857)
XLA Ops:
  0.6 34.1 %smoother.1 = (f32[1,8,8,8,128]{4,3,2,1,0:T(8,128)S(1)}, f32[1,8,17]{2,1,0:T(8,128)S(1)}) custom-call(f32[1,8,8,8,128]{4,3,2,1,0:T(8,128)} %load_hbm.1, f32[1,8,8,8,128]{4,3,2,1,0:T(8,128)} %mob_hbm.1, f32[3,1,8,16]{3,2,1,0:T(8,128)} %met_hbm.1, f32[5,8,128]{2,1,0:T(8,128)} %constant.2.clone.tab_hbm), custom_call_target="tpu_custom_call" | custom-call | tf_op jit(solution)/shard_map/smoother/pallas_call | solution.py:456
  34.7 0.7 %copy.8 = f32[1,8,8,8,128]{4,3,2,1,0:T(8,128)} copy(f32[1,8,8,8,128]{4,3,2,1,0:T(8,128)S(1)} %get-tuple-element.2) | data formatting | bytes 524288
  35.4 0.6 %copy.9 = f32[1,8,17]{2,1,0:T(8,128)} copy(f32[1,8,17]{2,1,0:T(8,128)S(1)} %get-tuple-element.3) | data formatting | bytes 1088

commit v4 on v3

--- a/solution.py
+++ b/solution.py
@@ -75,16 +75,17 @@
     return terms[0]
 
 
-def apply_line(matrix, v, sign):
-    pair = [(v[m], v[7 - m]) for m in range(4)]
-    even = [x if y is None else x + y for x, y in pair]
-    odd = [x if y is None else x - y for x, y in pair]
+def apply_line(matrix, v, sign, rows=range(4)):
+    even, odd = {}, {}
+    for m in range(4):
+        x, y = v[m], v[7 - m]
+        if x is not None or y is not None:
+            even[m] = x if y is None else x + y
+            odd[m] = x if y is None else x - y
     out = [None] * 8
-    for a in range(4):
-        with_even = total(
-            [float((matrix[a, m] + matrix[a, 7 - m]) / 2) * even[m] for m in range(4)]
-        )
-        with_odd = total([float((matrix[a, m] - matrix[a, 7 - m]) / 2) * odd[m] for m in range(4)])
+    for a in rows:
+        with_even = total([float((matrix[a, m] + matrix[a, 7 - m]) / 2) * e for m, e in even.items()])
+        with_odd = total([float((matrix[a, m] - matrix[a, 7 - m]) / 2) * o for m, o in odd.items()])
         out[a] = with_odd + with_even
         out[7 - a] = with_odd - with_even if sign < 0 else with_even - with_odd
     return out
@@ -106,7 +107,7 @@
     load_hbm, mob_hbm, met_hbm, tab_hbm,
     press_ref, coarse_ref,
     load_v, mob_v, met_v, tab_v, mats,
-    fx, fy, fz, dg, inv, rhs, fs, kv, zz, gx, gy, gz, k7,
+    fx, fy, fz, dg, inv, rhs, fs, kv, zz, gx, gy, gz, k0, k7, ky0, ky7,
     hold, sya, sg, sgx, sk, syb, sye, syc, sc,
     rxl, rxd, rxg, rxgx, rya, rca, rk, rxb, ryb, rcb, rc,
     local_sem, send_sem, recv_sem,
@@ -116,18 +117,20 @@
     dn, dp = lax.rem(d + 1, nd), lax.rem(d + nd - 1, nd)
     sn, sp = lax.rem(s + 1, ns), lax.rem(s + ns - 1, ns)
 
+    barrier = pltpu.get_barrier_semaphore()
+    around = [(dp, sp), (dp, sn), (dn, sp), (dn, sn), (dp, s), (dn, s), (d, sp), (d, sn)]
+    for device in around:
+        pl.semaphore_signal(barrier, inc=1, device_id=device, device_id_type=MESH)
     fetch = [
         pltpu.make_async_copy(met_hbm, met_v, local_sem.at[0]),
         pltpu.make_async_copy(tab_hbm, tab_v, local_sem.at[1]),
-        pltpu.make_async_copy(mob_hbm.at[0], mob_v, local_sem.at[2]),
-        pltpu.make_async_copy(load_hbm.at[0], load_v, local_sem.at[3]),
-    ]
+    ]
+    fetch += [
+        pltpu.make_async_copy(mob_hbm.at[0, i], mob_v.at[i], local_sem.at[2 + i]) for i in range(8)
+    ]
+    fetch.append(pltpu.make_async_copy(load_hbm.at[0], load_v, local_sem.at[10]))
     for copy in fetch:
         copy.start()
-    barrier = pltpu.get_barrier_semaphore()
-    around = [(a, b) for a in (dp, d, dn) for b in (sp, s, sn) if not (a is d and b is s)]
-    for device in around:
-        pl.semaphore_signal(barrier, inc=1, device_id=device, device_id_type=MESH)
 
     lane = lax.broadcasted_iota(jnp.int32, (8, 128), 1)
     sub8 = lax.broadcasted_iota(jnp.int32, (8, 128), 0)
@@ -169,8 +172,8 @@
     ).reshape(3, 8, 128)
     base = [spread[n] * tab_v[0] for n in range(3)]
 
-    fetch[2].wait()
     for i in range(8):
+        fetch[2 + i].wait()
         for j in range(8):
             m = mob_v[i, :, j, :] * float(WEIGHTS[i] * WEIGHTS[j])
             fx[i, j] = m * base[0]
@@ -180,18 +183,30 @@
                 sg[j] = m
     sg[8] = base[1]
     sg[9] = base[2]
-    zz[...] = wide_dot(fz[...].reshape(512, 128), mats[2]).reshape(8, 8, 8, 128)
-    squared = DERIV * DERIV
-    for j in range(8):
-        line = apply_line(squared.T, [fx[i, j] for i in range(8)], 1)
+    squared = (DERIV * DERIV).T
+
+    def z_diagonal(at):
+        shape = fz[at].shape
+        zz[at] = wide_dot(fz[at].reshape(-1, 128), mats[2]).reshape(shape)
+
+    z_diagonal(slice(0, 1))
+    z_diagonal(slice(7, 8))
+    z_diagonal((slice(1, 7), 0))
+    z_diagonal((slice(1, 7), 7))
+    for j in range(8):
+        ends = range(4) if j in (0, 7) else (0,)
+        line = apply_line(squared, [fx[i, j] for i in range(8)], 1, ends)
         for i in range(8):
-            dg[i, j] = line[i] + zz[i, j]
+            if line[i] is not None:
+                dg[i, j] = line[i] + zz[i, j]
         sg[10 + j] = line[7]
     for i in range(8):
-        line = apply_line(squared.T, [fy[i, j] for j in range(8)], 1)
+        ends = range(4) if i in (0, 7) else (0,)
+        line = apply_line(squared, [fy[i, j] for j in range(8)], 1, ends)
         for j in range(8):
-            dg[i, j] = dg[i, j] + line[j]
-    fetch[3].wait()
+            if line[j] is not None:
+                dg[i, j] = dg[i, j] + line[j]
+    fetch[10].wait()
     sya[0, 0] = load_v[:, 7, 7, :]
     sya[1, 0] = load_v[:, 0, 0, :]
     sya[0, 1] = dg[:, 7, 7, :]
@@ -253,6 +268,16 @@
                 out[i, j] = v
         return out
 
+    z_diagonal((slice(1, 7), slice(1, 7)))
+    for j in inner:
+        line = apply_line(squared, [fx[i, j] for i in range(8)], 1, (1, 2, 3))
+        for i in inner:
+            dg[i, j] = line[i] + zz[i, j]
+    for i in inner:
+        line = apply_line(squared, [fy[i, j] for j in range(8)], 1, (1, 2, 3))
+        for j in inner:
+            dg[i, j] = dg[i, j] + line[j]
+
     for j in range(8):
         line = [fx[a, j] for a in range(8)]
         for i in range(7):
@@ -277,6 +302,33 @@
 
     for i, j in deep:
         first_step(i, j, load_v[i, :, j, :], dg[i, j])
+
+    def z_part(at):
+        shape = fs[at].shape
+        flux = wide_dot(fs[at].reshape(-1, 128), mats[0]) * fz[at].reshape(-1, 128)
+        zz[at] = wide_dot(flux, mats[1]).reshape(shape)
+
+    def column(line, m, n):
+        return total([float(DERIV[a, m] * DERIV[a, n]) * line[a] for a in range(8)])
+
+    z_part((slice(1, 7), slice(1, 7)))
+    for j in inner:
+        grad = apply_line(DERIV, [None] + [fs[i, j] for i in inner] + [None], -1)
+        line = apply_line(DERIV.T, [fx[i, j] * grad[i] for i in range(8)], -1)
+        for i in range(8):
+            kv[i, j] = line[i]
+        line = [fx[a, j] for a in range(8)]
+        for i in range(8):
+            k0[i, j] = column(line, i, 0)
+    for i in inner:
+        grad = apply_line(DERIV, [None] + [fs[i, j] for j in inner] + [None], -1)
+        line = apply_line(DERIV.T, [fy[i, j] * grad[j] for j in range(8)], -1)
+        for j in range(8):
+            kv[i, j] = (kv[i, j] + (line[j] + zz[i, j])) if j in inner else line[j]
+        line = [fy[i, b] for b in range(8)]
+        for j in range(8):
+            ky0[i, j] = column(line, j, 0)
+            ky7[i, j] = column(line, j, 7)
 
     def low_high(v):
         plain = total(v)
@@ -316,10 +368,15 @@
         first[n].wait_recv()
     start_rim((0,))
     for j in range(8):
-        grad = apply_line(DERIV, [fs[i, j] for i in range(7)] + [None], -1)
-        line = apply_line(DERIV.T, [fx[i, j] * grad[i] for i in range(8)], -1)
-        for i in range(8):
-            kv[i, j] = line[i]
+        if j in inner:
+            v = fs[0, j]
+            for i in range(8):
+                kv[i, j] = kv[i, j] + k0[i, j] * v
+        else:
+            grad = apply_line(DERIV, [fs[i, j] for i in range(7)] + [None], -1)
+            line = apply_line(DERIV.T, [fx[i, j] * grad[i] for i in range(8)], -1)
+            for i in range(8):
+                kv[i, j] = (kv[i, j] + line[i]) if i in inner else line[i]
     sye[0] = kv[:, 7, 7, :]
     sye[1] = kv[:, 0, 0, :]
     second = [
@@ -328,23 +385,22 @@
         send(kv.at[7], rxb.at[0], (dn, s)),
     ]
 
-    def yz_part(low, high):
-        rows = 64 * (high - low)
-        flux = wide_dot(fs[low:high].reshape(rows, 128), mats[0]) * fz[low:high].reshape(rows, 128)
-        zz[low:high] = wide_dot(flux, mats[1]).reshape(high - low, 8, 8, 128)
-        for i in range(low, high):
-            grad = apply_line(DERIV, [fs[i, j] for j in range(8)], -1)
-            line = apply_line(DERIV.T, [fy[i, j] * grad[j] for j in range(8)], -1)
-            for j in range(8):
-                kv[i, j] = kv[i, j] + (line[j] + zz[i, j])
-
-    yz_part(1, 7)
+    z_part((slice(1, 7), 0))
+    z_part((slice(1, 7), 7))
+    for i in inner:
+        low, high = fs[i, 0], fs[i, 7]
+        for j in range(8):
+            value = kv[i, j] + (ky0[i, j] * low + ky7[i, j] * high)
+            kv[i, j] = value if j in inner else value + zz[i, j]
     first[10].wait_recv()
     for j in range(8):
         fy[0, j] = fy[0, j] + rxg[j] * rxg[8]
         fz[0, j] = fz[0, j] + rxg[j] * rxg[9]
-        kv[0, j] = kv[0, j] + rxg[10 + j] * fs[0, j]
-    yz_part(0, 1)
+    z_part(slice(0, 1))
+    grad = apply_line(DERIV, [fs[0, j] for j in range(8)], -1)
+    line = apply_line(DERIV.T, [fy[0, j] * grad[j] for j in range(8)], -1)
+    for j in range(8):
+        kv[0, j] = kv[0, j] + rxg[10 + j] * fs[0, j] + (line[j] + zz[0, j])
     syb[0] = kv[:, 7, 7, :]
     syb[1] = kv[:, 0, 0, :]
     second += [send(syb.at[0], ryb.at[0], (d, sn)), send(syb.at[1], ryb.at[1], (d, sp))]
@@ -449,11 +505,23 @@
         copy.wait_send()
 
 
+def write_out(pressure_ref, coarse_ref, pressure_hbm, coarse_hbm, sem):
+    copies = [pltpu.make_async_copy(coarse_ref, coarse_hbm, sem.at[8])]
+    copies += [
+        pltpu.make_async_copy(pressure_ref.at[0, i], pressure_hbm.at[0, i], sem.at[i])
+        for i in range(8)
+    ]
+    for copy in copies:
+        copy.start()
+    for copy in copies:
+        copy.wait()
+
+
 def shards(element_load, mobility, metric):
     field = pltpu.VMEM((8, 8, 8, 128), F32)
     hbm = pl.BlockSpec(memory_space=pltpu.HBM)
     vmem = pl.BlockSpec(memory_space=pltpu.VMEM)
-    return pl.pallas_call(
+    pressure, coarse = pl.pallas_call(
         kernel,
         name="smoother",
         out_shape=(
@@ -467,7 +535,7 @@
             pltpu.VMEM((3, 1, 8, 16), F32),
             pltpu.VMEM((5, 8, 128), F32),
             pltpu.VMEM((5, 256, 256), BF16),
-            *[field] * 13,
+            *[field] * 16,
             pltpu.VMEM((4, 8, 128), F32),
             pltpu.VMEM((2, 2, 8, 128), F32),
             pltpu.VMEM((18, 8, 128), F32),
@@ -488,12 +556,26 @@
             pltpu.VMEM((2, 8, 128), F32),
             pltpu.VMEM((4, 8, 128), F32),
             pltpu.VMEM((3, 8, 128), F32),
-            pltpu.SemaphoreType.DMA((4,)),
+            pltpu.SemaphoreType.DMA((11,)),
             pltpu.SemaphoreType.DMA((25,)),
             pltpu.SemaphoreType.DMA((25,)),
         ],
         compiler_params=pltpu.CompilerParams(collective_id=0, has_side_effects=True),
     )(element_load, mobility, metric, jnp.asarray(small_tables()))
+    return pl.pallas_call(
+        write_out,
+        name="write_out",
+        out_shape=(
+            jax.ShapeDtypeStruct(pressure.shape, F32),
+            jax.ShapeDtypeStruct(coarse.shape, F32),
+        ),
+        in_specs=[vmem, vmem],
+        out_specs=(hbm, hbm),
+        scratch_shapes=[pltpu.SemaphoreType.DMA((9,))],
+    )(
+        pltpu.with_memory_space_constraint(pressure, pltpu.VMEM),
+        pltpu.with_memory_space_constraint(coarse, pltpu.VMEM),
+    )
 
 
 def solution(mesh):

time: 36.2 us -> 35.7 us (0.986)
  local copies, waits for them, and re-layouts: 1.3 us -> 0 us
  Pallas kernels: 34.1 us -> 34.9 us
    unnamed x2 -> x0, local copies, waits for them, and re-layouts: 1.3 us -> none
    pallas_call x0 -> x1, Pallas kernels: none -> 0.77 us  [shards(): pl.pallas_call(write_out, name='write_out', out_shape=(jax.ShapeDtypeStru...]
where the time goes in v4:
time: 35.7 us; the launch traced here: 35.5 us
  Pallas kernels  34.9 us (98%)
  between operations  0.64 us (2%)
    pallas_call x1, Pallas kernels, shards(): pl.pallas_call(kernel, name='smoother', out_shape=(pltpu.VMEM((1, 8, 8, 8...  34.1 us
    pallas_call x1, Pallas kernels, shards(): pl.pallas_call(write_out, name='write_out', out_shape=(jax.ShapeDtypeStru...  0.77 us

profile of v4, /device:TPU:1, one launch (start us, length us, event | category | flops | bytes accessed | tf_op | source)
XLA Modules:
  0.0 35.5 jit_solution(4989384022196385349)
XLA Ops:
  0.6 34.1 %smoother.1 = (f32[1,8,8,8,128]{4,3,2,1,0:T(8,128)S(1)}, f32[1,8,17]{2,1,0:T(8,128)S(1)}) custom-call(f32[1,8,8,8,128]{4,3,2,1,0:T(8,128)} %load_hbm.1, f32[1,8,8,8,128]{4,3,2,1,0:T(8,128)} %mob_hbm.1, f32[3,1,8,16]{3,2,1,0:T(8,128)} %met_hbm.1, f32[5,8,128]{2,1,0:T(8,128)} %constant.2.clone.tab_hbm), custom_call_target="tpu_custom_call" | custom-call | tf_op jit(solution)/shard_map/smoother/pallas_call | solution.py:524
  34.7 0.8 %write_out.1 = (f32[1,8,8,8,128]{4,3,2,1,0:T(8,128)}, f32[1,8,17]{2,1,0:T(8,128)}) custom-call(f32[1,8,8,8,128]{4,3,2,1,0:T(8,128)S(1)} %get-tuple-element.4.pressure_ref, f32[1,8,17]{2,1,0:T(8,128)S(1)} %get-tuple-element.5.coarse_ref), custom_call_target="tpu_custom_call" | custom-call | tf_op jit(solution)/shard_map/write_out/pallas_call | solution.py:565

commit v5 on v4

--- a/solution.py
+++ b/solution.py
@@ -108,7 +108,7 @@
     press_ref, coarse_ref,
     load_v, mob_v, met_v, tab_v, mats,
     fx, fy, fz, dg, inv, rhs, fs, kv, zz, gx, gy, gz, k0, k7, ky0, ky7,
-    hold, sya, sg, sgx, sk, syb, sye, syc, sc,
+    hold, sya, sca, sg, sgx, sk, syb, sye, syc, sc,
     rxl, rxd, rxg, rxgx, rya, rca, rk, rxb, ryb, rcb, rc,
     local_sem, send_sem, recv_sem,
 ):
@@ -126,9 +126,12 @@
         pltpu.make_async_copy(tab_hbm, tab_v, local_sem.at[1]),
     ]
     fetch += [
-        pltpu.make_async_copy(mob_hbm.at[0, i], mob_v.at[i], local_sem.at[2 + i]) for i in range(8)
-    ]
-    fetch.append(pltpu.make_async_copy(load_hbm.at[0], load_v, local_sem.at[10]))
+        pltpu.make_async_copy(
+            mob_hbm.at[0, pl.ds(4 * h, 4)], mob_v.at[pl.ds(4 * h, 4)], local_sem.at[2 + h]
+        )
+        for h in range(2)
+    ]
+    fetch.append(pltpu.make_async_copy(load_hbm.at[0], load_v, local_sem.at[4]))
     for copy in fetch:
         copy.start()
 
@@ -173,7 +176,8 @@
     base = [spread[n] * tab_v[0] for n in range(3)]
 
     for i in range(8):
-        fetch[2 + i].wait()
+        if i % 4 == 0:
+            fetch[2 + i // 4].wait()
         for j in range(8):
             m = mob_v[i, :, j, :] * float(WEIGHTS[i] * WEIGHTS[j])
             fx[i, j] = m * base[0]
@@ -206,11 +210,14 @@
         for j in range(8):
             if line[j] is not None:
                 dg[i, j] = dg[i, j] + line[j]
-    fetch[10].wait()
+    fetch[4].wait()
     sya[0, 0] = load_v[:, 7, 7, :]
     sya[1, 0] = load_v[:, 0, 0, :]
     sya[0, 1] = dg[:, 7, 7, :]
     sya[1, 1] = dg[:, 0, 0, :]
+    for slot, (end, i) in enumerate(((0, 7), (1, 7), (0, 0), (1, 0))):
+        for field in range(2):
+            sca[slot, field : field + 1] = sya[end, field, i : i + 1]
 
     used = [0]
 
@@ -226,10 +233,10 @@
 
     pl.semaphore_wait(barrier, 8)
     first = [
-        send(sya.at[0], rca.at[0], (dn, sn)),
-        send(sya.at[1], rca.at[1], (dn, sp)),
-        send(sya.at[0], rca.at[2], (dp, sn)),
-        send(sya.at[1], rca.at[3], (dp, sp)),
+        send(sca.at[0], rca.at[0], (dn, sn)),
+        send(sca.at[1], rca.at[1], (dn, sp)),
+        send(sca.at[2], rca.at[2], (dp, sn)),
+        send(sca.at[3], rca.at[3], (dp, sp)),
         send(sya.at[0], rya.at[0], (d, sn)),
         send(sya.at[1], rya.at[1], (d, sp)),
         send(dg.at[7], rxd.at[0], (dn, s)),
@@ -349,24 +356,21 @@
             lambda i, j: load_v[i, :, j, :],
             lambda side, j: rxl[side, :, j, :],
             lambda side, i: wide(rya[side, 0, i : i + 1, :]),
-            lambda slot, i: wide(rca[slot, 0, i : i + 1, :]),
+            lambda slot, i: wide(rca[slot, 0:1, :]),
         )
         diags = rim_sums(
             planes_i,
             lambda i, j: dg[i, j],
             lambda side, j: rxd[side, j],
             lambda side, i: wide(rya[side, 1, i : i + 1, :]),
-            lambda slot, i: wide(rca[slot, 1, i : i + 1, :]),
+            lambda slot, i: wide(rca[slot, 1:2, :]),
         )
         for i, j in loads:
             first_step(i, j, loads[i, j], diags[i, j])
 
-    for n in (4, 5):
+    for n in (4, 5, 6, 8, 0, 1):
         first[n].wait_recv()
-    start_rim(inner)
-    for n in (0, 1, 6, 8):
-        first[n].wait_recv()
-    start_rim((0,))
+    start_rim(range(7))
     for j in range(8):
         if j in inner:
             v = fs[0, j]
@@ -461,18 +465,28 @@
         inside, edge = both[0:8], pltpu.roll(both[8:16], 1, 0)
         return inside + jnp.where(sub8 == 0, 0.0, edge), jnp.where(sub8 == 0, edge, 0.0)
 
-    for n in (3, 4):
+    x_deep = {j: total([gx[i, j] * fs[i, j] for i in inner]) for j in inner}
+    y_deep = {i: total([gy[i, j] * fs[i, j] for j in inner]) for i in inner}
+    z_deep = {}
+    for i in inner:
+        terms = {j: gz[i, j] * fs[i, j] for j in inner}
+        z_deep[i] = [total([weight[q][j] * v for j, v in terms.items()]) for q in range(2)]
+    for n in (2, 0, 1, 3, 4):
         second[n].wait_recv()
-    finish(inner)
-    for n in (0, 1, 2):
-        second[n].wait_recv()
-    finish((0,))
-    x_sum = [total([gx[i, j] * fs[i, j] for i in range(7)]) for j in range(8)]
-    y_sum = [total([gy[i, j] * fs[i, j] for j in range(8)]) for i in range(7)]
-    z_line = []
+    finish(range(7))
+    x_sum, y_sum, z_line = [], [], []
+    for j in range(8):
+        deep_part = x_deep[j] if j in inner else total([gx[i, j] * fs[i, j] for i in inner])
+        x_sum.append(deep_part + gx[0, j] * fs[0, j])
     for i in range(7):
-        terms = [gz[i, j] * fs[i, j] for j in range(8)]
-        z_line.append([weigh(terms, q) for q in range(2)])
+        if i in inner:
+            low, high = gz[i, 0] * fs[i, 0], gz[i, 7] * fs[i, 7]
+            y_sum.append(y_deep[i] + (gy[i, 0] * fs[i, 0] + gy[i, 7] * fs[i, 7]))
+            z_line.append([z_deep[i][0] + 0.25 * low, z_deep[i][1] + 0.25 * high])
+        else:
+            y_sum.append(total([gy[i, j] * fs[i, j] for j in range(8)]))
+            terms = [gz[i, j] * fs[i, j] for j in range(8)]
+            z_line.append([weigh(terms, q) for q in range(2)])
     y_high = weigh(y_sum, 1)
     plain = [
         hold[2] - weigh(x_sum, 0) + y_high,
@@ -538,6 +552,7 @@
             *[field] * 16,
             pltpu.VMEM((4, 8, 128), F32),
             pltpu.VMEM((2, 2, 8, 128), F32),
+            pltpu.VMEM((4, 2, 128), F32),
             pltpu.VMEM((18, 8, 128), F32),
             pltpu.VMEM((8, 8, 128), F32),
             pltpu.VMEM((2, 8, 128), F32),
@@ -550,13 +565,13 @@
             pltpu.VMEM((18, 8, 128), F32),
             pltpu.VMEM((8, 8, 128), F32),
             pltpu.VMEM((2, 2, 8, 128), F32),
-            pltpu.VMEM((4, 2, 8, 128), F32),
+            pltpu.VMEM((4, 2, 128), F32),
             pltpu.VMEM((2, 8, 128), F32),
             pltpu.VMEM((2, 8, 8, 128), F32),
             pltpu.VMEM((2, 8, 128), F32),
             pltpu.VMEM((4, 8, 128), F32),
             pltpu.VMEM((3, 8, 128), F32),
-            pltpu.SemaphoreType.DMA((11,)),
+            pltpu.SemaphoreType.DMA((5,)),
             pltpu.SemaphoreType.DMA((25,)),
             pltpu.SemaphoreType.DMA((25,)),
         ],

time: 35.7 us -> 35.4 us (level)
  no operation moved by 1% of the time
where the time goes in v5:
time: 35.4 us; the launch traced here: 35.2 us
  Pallas kernels  34.6 us (98%)
  between operations  0.64 us (2%)
    pallas_call x1, Pallas kernels, shards(): pl.pallas_call(kernel, name='smoother', out_shape=(pltpu.VMEM((1, 8, 8, 8...  33.8 us
    pallas_call x1, Pallas kernels, shards(): pl.pallas_call(write_out, name='write_out', out_shape=(jax.ShapeDtypeStru...  0.77 us

profile of v5, /device:TPU:1, one launch (start us, length us, event | category | flops | bytes accessed | tf_op | source)
XLA Modules:
  0.0 35.2 jit_solution(10778666465555191286)
XLA Ops:
  0.6 33.8 %smoother.1 = (f32[1,8,8,8,128]{4,3,2,1,0:T(8,128)S(1)}, f32[1,8,17]{2,1,0:T(8,128)S(1)}) custom-call(f32[1,8,8,8,128]{4,3,2,1,0:T(8,128)} %load_hbm.1, f32[1,8,8,8,128]{4,3,2,1,0:T(8,128)} %mob_hbm.1, f32[3,1,8,16]{3,2,1,0:T(8,128)} %met_hbm.1, f32[5,8,128]{2,1,0:T(8,128)} %constant.2.clone.tab_hbm), custom_call_target="tpu_custom_call" | custom-call | tf_op jit(solution)/shard_map/smoother/pallas_call | solution.py:538
  34.5 0.8 %write_out.1 = (f32[1,8,8,8,128]{4,3,2,1,0:T(8,128)}, f32[1,8,17]{2,1,0:T(8,128)}) custom-call(f32[1,8,8,8,128]{4,3,2,1,0:T(8,128)S(1)} %get-tuple-element.4.pressure_ref, f32[1,8,17]{2,1,0:T(8,128)S(1)} %get-tuple-element.5.coarse_ref), custom_call_target="tpu_custom_call" | custom-call | tf_op jit(solution)/shard_map/write_out/pallas_call | solution.py:580

commit v6 on v5

--- a/solution.py
+++ b/solution.py
@@ -232,19 +232,20 @@
         return copy
 
     pl.semaphore_wait(barrier, 8)
-    first = [
-        send(sca.at[0], rca.at[0], (dn, sn)),
-        send(sca.at[1], rca.at[1], (dn, sp)),
-        send(sca.at[2], rca.at[2], (dp, sn)),
-        send(sca.at[3], rca.at[3], (dp, sp)),
-        send(sya.at[0], rya.at[0], (d, sn)),
-        send(sya.at[1], rya.at[1], (d, sp)),
-        send(dg.at[7], rxd.at[0], (dn, s)),
-        send(dg.at[0], rxd.at[1], (dp, s)),
-        send(load_hbm.at[0, 7], rxl.at[0], (dn, s)),
-        send(load_hbm.at[0, 0], rxl.at[1], (dp, s)),
-        send(sg, rxg, (dn, s)),
-    ]
+    sent = {
+        0: send(sca.at[0], rca.at[0], (dn, sn)),
+        1: send(sca.at[1], rca.at[1], (dn, sp)),
+        4: send(sya.at[0], rya.at[0], (d, sn)),
+        5: send(sya.at[1], rya.at[1], (d, sp)),
+        6: send(dg.at[7], rxd.at[0], (dn, s)),
+        8: send(load_hbm.at[0, 7], rxl.at[0], (dn, s)),
+        2: send(sca.at[2], rca.at[2], (dp, sn)),
+        3: send(sca.at[3], rca.at[3], (dp, sp)),
+        10: send(sg, rxg, (dn, s)),
+        7: send(dg.at[0], rxd.at[1], (dp, s)),
+        9: send(load_hbm.at[0, 0], rxl.at[1], (dp, s)),
+    }
+    first = [sent[n] for n in range(11)]
 
     inner = range(1, 7)
     rim = [(i, j) for i in range(8) for j in range(8) if i in (0, 7) or j in (0, 7)]

time: 35.4 us -> 35.4 us (level)
  no operation moved by 1% of the time
where the time goes in v6:
time: 35.4 us; the launch traced here: 35.3 us
  Pallas kernels  34.6 us (98%)
  between operations  0.64 us (2%)
    pallas_call x1, Pallas kernels, shards(): pl.pallas_call(kernel, name='smoother', out_shape=(pltpu.VMEM((1, 8, 8, 8...  33.8 us
    pallas_call x1, Pallas kernels, shards(): pl.pallas_call(write_out, name='write_out', out_shape=(jax.ShapeDtypeStru...  0.77 us

profile of v6, /device:TPU:1, one launch (start us, length us, event | category | flops | bytes accessed | tf_op | source)
XLA Modules:
  0.0 35.3 jit_solution(5149773698763129855)
XLA Ops:
  0.6 33.8 %smoother.1 = (f32[1,8,8,8,128]{4,3,2,1,0:T(8,128)S(1)}, f32[1,8,17]{2,1,0:T(8,128)S(1)}) custom-call(f32[1,8,8,8,128]{4,3,2,1,0:T(8,128)} %load_hbm.1, f32[1,8,8,8,128]{4,3,2,1,0:T(8,128)} %mob_hbm.1, f32[3,1,8,16]{3,2,1,0:T(8,128)} %met_hbm.1, f32[5,8,128]{2,1,0:T(8,128)} %constant.2.clone.tab_hbm), custom_call_target="tpu_custom_call" | custom-call | tf_op jit(solution)/shard_map/smoother/pallas_call | solution.py:539
  34.5 0.8 %write_out.1 = (f32[1,8,8,8,128]{4,3,2,1,0:T(8,128)}, f32[1,8,17]{2,1,0:T(8,128)}) custom-call(f32[1,8,8,8,128]{4,3,2,1,0:T(8,128)S(1)} %get-tuple-element.4.pressure_ref, f32[1,8,17]{2,1,0:T(8,128)S(1)} %get-tuple-element.5.coarse_ref), custom_call_target="tpu_custom_call" | custom-call | tf_op jit(solution)/shard_map/write_out/pallas_call | solution.py:581
